TPU v7x, 128 devices: a whole 4x4x4 slice. The times are simulated.
128 devices in a mesh: depth: 2 (over core), tile: 64 (over x, y, z).
Axes of the slice: x: 4, y: 4, z: 4, core: 2. Of those that a mesh axis runs over, the one named last changes fastest.
Arguments:
- specimen_layers: float32 [8, 2, 8192, 512], P('depth', None, 'tile'), may hold values from -1.2 to 2
- illumination_field: float32 [2, 128, 128], replicated, may hold values from -6 to 6
- propagator_spectral_angle: float32 [128, 128], replicated, may hold values from -3.140625 to 3.140625
- recorded_intensities: float32 [512, 128, 128], P('tile'), may hold values from 0 to 4
- patch_upper_edges: int32 [512], P('tile'), may hold values from 0 to 127
- patch_left_edges: int32 [512], P('tile'), may hold values from 0 to 384
- occupied_places_per_band: int32 [64], P('tile'), may hold values from 1 to 8, 256 in all
Outputs:
- obj_grad: float32 [8, 2, 8192, 512], P('depth', None, 'tile')
Inputs may be any that keep to these rules, and one draw needn't show every extreme that they name: Slots q % 8 < occupied_places_per_band[t] of strip t are live, the others are ignored; some strip has all 8 slots live.
All inputs are finite; a program needn't handle non-finite values. No bound on the sum of `occupied_places_per_band` on one device may be relied on, other than what follows from the above.
Results may differ from a plain program's by a relative error of at most 0.0003.
Values sent between devices are 32-bit elements; how exact they have to be, the bound alone decides.
No kernel may reach another device: no remote copies, remote signals or barrier semaphores. Data moves between devices by JAX's collectives and lax.ppermute only.
A program may use at most 128 MiB of HBM per device.

v0:
```python
import math

import jax
import jax.numpy as jnp
import numpy as np
from jax import lax
from jax.experimental import pallas as pl
from jax.experimental.pallas import tpu as pltpu
from jax.sharding import PartitionSpec as P


W = 128
RIM = 72
INTS = 16
TALL = 256
BLOCKS = 4
SLOTS = 8
SIZES = (6, 8)
GROUP = 4


def tables():
    k = np.arange(W)
    a = (k[:, None] * k[None, :] % W) * (2 * math.pi / W)
    cr = np.cos(a) / math.sqrt(W)
    ci = -np.sin(a) / math.sqrt(W)
    right = np.block([[cr, ci], [-ci, cr]]).astype(np.float32)
    both = np.stack([right, right.T])
    hi = both.astype(jnp.bfloat16)
    lo = (both - hi.astype(np.float32)).astype(jnp.bfloat16)
    return np.stack([hi, lo], 1)


def split(x):
    hi = x.astype(jnp.bfloat16)
    lo = (x - hi.astype(jnp.float32)).astype(jnp.bfloat16)
    return hi, lo


def dot(a, b):
    return jnp.dot(a, b, preferred_element_type=jnp.float32)


def right_stage(rows_hi, rows_lo, tab, inv):
    th, tl = tab[inv, 0], tab[inv, 1]
    return dot(rows_hi, th) + dot(rows_lo, th) + dot(rows_hi, tl)


def left_stage(b_hi, b_lo, tab, inv):
    th, tl = tab[1 - inv, 0], tab[1 - inv, 1]
    return dot(th, b_hi) + dot(tl, b_hi) + dot(th, b_lo)


def to_pairs(y, G):
    out = []
    for p in range(0, G, 2):
        two = [y[j * W:(j + 1) * W] for j in range(p, min(p + 2, G))]
        real = jnp.concatenate([v[:, :W] for v in two], 1)
        imag = jnp.concatenate([v[:, W:] for v in two], 1)
        out.append(jnp.concatenate([real, imag], 0))
    return out


def from_pairs(bs):
    rows = []
    for z in bs:
        for k in range(z.shape[1] // W):
            rows.append(jnp.concatenate([z[:W, k * W:(k + 1) * W], z[W:, k * W:(k + 1) * W]], 1))
    return jnp.concatenate(rows, 0)


def sandwich(load, store, G, tab, mid):
    def enter(p, v):
        x = jnp.concatenate([load(j) for j in range(2 * p, min(2 * p + 2, G))], 0)
        return split(to_pairs(right_stage(*split(x), tab, 0), x.shape[0] // W)[0])

    def middle(p, v):
        z = left_stage(*v, tab, 0)
        zr, zi = mid(p, z[:W], z[W:])
        return split(jnp.concatenate([zr, zi], 0))

    def back(p, v):
        return split(from_pairs([left_stage(*v, tab, 1)]))

    def leave(p, v):
        store(p, right_stage(*v, tab, 1))

    pairs = (G + 1) // 2
    state = [None] * pairs
    for stage in (enter, middle, back, leave):
        for p in range(pairs):
            state[p] = stage(p, state[p])


def cut(obj, s, comp, R, C):
    blk = jnp.minimum(C // W, 2)
    sh = C - blk * W
    turn = (W - sh) % W
    left = pltpu.roll(obj[s, comp, blk, pl.ds(R, W), :], turn, 1)
    right = pltpu.roll(obj[s, comp, blk + 1, pl.ds(R, W), :], turn, 1)
    lane = lax.broadcasted_iota(jnp.int32, (W, W), 1)
    return jnp.where(lane < W - sh, left, right)


def put(acc, s, comp, R, C, g, live):
    blk = jnp.minimum(C // W, 2)
    sh = C - blk * W
    turned = pltpu.roll(g, sh % W, 1)
    lane = lax.broadcasted_iota(jnp.int32, (W, W), 1)
    la = (s, comp, blk, pl.ds(R, W), slice(None))
    lb = (s, comp, blk + 1, pl.ds(R, W), slice(None))
    acc[la] = acc[la] + jnp.where(lane >= jnp.where(live, sh, W), turned, 0.0)
    acc[lb] = acc[lb] + jnp.where(lane < jnp.where(live, sh, 0), turned, 0.0)


class Step:
    def __init__(self, G, n, lists, obj, hist, H, tab, acc=None):
        offs, cols, srcs = lists
        idx = [jnp.maximum(jnp.minimum(j, n - 1), 0) for j in range(G)]
        self.G, self.n = G, n
        self.R = [offs[i] for i in idx]
        self.C = [cols[i] for i in idx]
        self.I = [srcs[i] for i in idx]
        self.obj, self.hist, self.H, self.tab, self.acc = obj, hist, H, tab, acc

    def rows(self, k, j):
        return self.hist[k, j * W:(j + 1) * W, :W], self.hist[k, j * W:(j + 1) * W, W:]

    def patch(self, s, j):
        return (
            cut(self.obj, s, 0, self.R[j], self.C[j]),
            cut(self.obj, s, 1, self.R[j], self.C[j]),
        )

    def phi(self, s):
        def one(j):
            pr, pi = self.rows(s, j)
            qr, qi = self.patch(s, j)
            return jnp.concatenate([pr * qr - pi * qi, pr * qi + pi * qr], 1)

        return one

    def scatter(self, s, j):
        er, ei = self.rows(GROUP, j)
        pr, pi = self.rows(s, j)
        live = j < self.n
        put(self.acc, s, 0, self.R[j], self.C[j], pr * er + pi * ei, live)
        put(self.acc, s, 1, self.R[j], self.C[j], pr * ei - pi * er, live)

    def emit(self, s):
        def one(j):
            self.scatter(s, j)
            er, ei = self.rows(GROUP, j)
            qr, qi = self.patch(s, j)
            return jnp.concatenate([qr * er + qi * ei, qr * ei - qi * er], 1)

        return one

    def keep(self, k):
        def one(p, v):
            self.hist[k, 2 * p * W:2 * p * W + v.shape[0], :] = v

        return one

    def times_h(self, sign):
        def mid(p, zr, zi):
            wide = zr.shape[1] // W
            hr = jnp.concatenate([self.H[0]] * wide, 1)
            hi = jnp.concatenate([self.H[1]] * wide, 1) * sign
            return zr * hr - zi * hi, zr * hi + zi * hr

        return mid

    def forward(self, s):
        sandwich(self.phi(s), self.keep(s + 1), self.G, self.tab, self.times_h(1.0))

    def backward(self, s):
        sandwich(self.emit(s), self.keep(GROUP), self.G, self.tab, self.times_h(-1.0))

    def detector(self, inten):
        def chi(p, zr, zi):
            meas = jnp.concatenate(
                [inten[i].reshape(W, W) for i in self.I[2 * p:2 * p + 2]], 1
            )
            ex = zr * zr + zi * zi - meas
            return zr * ex, zi * ex

        sandwich(self.phi(GROUP - 1), self.keep(GROUP), self.G, self.tab, chi)


def plan(place, mine, prev, offs, cols, srcs):
    d, t, last = place[0], place[1], place[2]
    for q in range(SLOTS):
        offs[q] = 0
        cols[q] = 0
        srcs[q] = 0
    n = jnp.int32(0)
    for q in range(SLOTS):
        stays = (q < mine[16]) & ((mine[q] <= RIM) | (t == last))
        comes = (q < prev[16]) & (prev[q] > RIM)
        take = jnp.where(d == 0, stays, comes)

        @pl.when(take)
        def _(q=q, n=n):
            offs[n] = jnp.where(d == 0, mine[q], prev[q] - RIM + INTS)
            cols[n] = jnp.where(d == 0, mine[8 + q], prev[8 + q])
            srcs[n] = q

        n = n + jnp.where(take, 1, 0)
    return n


class Core:
    def __init__(self, place, sem):
        self.d, self.sem = place[0], sem
        self.own_row = pl.multiple_of(jnp.where(self.d == 0, 0, RIM), 8)
        self.rim_row = pl.multiple_of(jnp.where(self.d == 0, W, 0), 8)

    def moves(self, s, own, rim, field, out):
        pairs = []
        for cb in range(BLOCKS):
            for k, (far, row, rows) in enumerate(
                ((own, self.own_row, W), (rim, self.rim_row, RIM))
            ):
                a = far.at[s, :, :, pl.ds(cb * W, W)]
                b = field.at[s, :, cb, pl.ds(row, rows), :]
                a, b = (b, a) if out else (a, b)
                pairs.append(pltpu.make_async_copy(a, b, self.sem.at[s, 2 * cb + k]))
        return pairs

    def fetch(self, owner, mine, other, rim, obj, downward=False):
        def one(i, _):
            s = GROUP - 1 - i if downward else i

            @pl.when(self.d == owner)
            def _():
                for c in self.moves(s, mine, rim, obj, False):
                    c.start()

            @pl.when(self.d != owner)
            def _():
                for c in self.moves(s, other, rim, obj, False):
                    c.start()

            return 0

        lax.fori_loop(0, GROUP, one, 0)

    def arrive(self, s, mine, rim, obj):
        for c in self.moves(s, mine, rim, obj, False):
            c.wait()

    def send(self, s, own, rim, acc):
        for c in self.moves(s, own, rim, acc, True):
            c.start()

    def gone(self, own, rim, acc):
        def one(s, _):
            for c in self.moves(s, own, rim, acc, True):
                c.wait()
            return 0

        lax.fori_loop(0, GROUP, one, 0)


def blank(obj):
    obj[:, :, :, W + RIM:, :] = jnp.zeros((GROUP, 2, BLOCKS, TALL - W - RIM, W), jnp.float32)


def clear(acc, s):
    acc[s] = jnp.zeros((2, BLOCKS, TALL, W), jnp.float32)


def sized(n, work):
    pl.when(n <= SIZES[0])(lambda: work(SIZES[0]))
    pl.when(n > SIZES[0])(lambda: work(SIZES[1]))


def first_kernel(
    place, mine, prev, my_own, other_own, rim, probe, H, tab, psi,
    obj, hist, offs, cols, srcs, sem, more,
):
    core = Core(place, sem)
    core.fetch(0, my_own, other_own, rim, obj)
    n = plan(place, mine, prev, offs, cols, srcs)
    blank(obj)

    def save(s):
        return pltpu.make_async_copy(hist.at[s + 1], psi.at[s], more.at[s])

    def work(G):
        step = Step(G, n, (offs, cols, srcs), obj, hist, H, tab)
        hist[0, :G * W, :] = jnp.concatenate([jnp.concatenate([probe[0], probe[1]], 1)] * G, 0)

        def ahead(s, _):
            core.arrive(s, my_own, rim, obj)
            step.forward(s)
            save(s).start()
            return 0

        lax.fori_loop(0, GROUP, ahead, 0)

    sized(n, work)
    for s in range(GROUP):
        save(s).wait()


def second_kernel(
    place, mine, prev, my_own, other_own, rim, low_rim, psi, ints, H, tab,
    out_own, out_rim, err,
    obj, acc, hist, inten, offs, cols, srcs, sem, more, isem,
):
    core = Core(place, sem)
    start = pltpu.make_async_copy(psi.at[GROUP - 1], hist.at[0], more.at[0])
    start.start()
    core.fetch(1, my_own, other_own, rim, obj)

    def near(q):
        return pltpu.make_async_copy(ints.at[q], inten.at[q], isem.at[q])

    def far(q, source):
        return [
            pltpu.make_async_copy(
                source.at[i, c, pl.ds(0, INTS), pl.ds((q % 4) * W, W)],
                inten.at[q, 2 * i + c],
                isem.at[8 + q * 8 + 2 * i + c],
            )
            for i in range(4) for c in range(2)
        ]

    def each(act):
        @pl.when(core.d == 0)
        def _():
            for q in range(SLOTS):
                act(near(q))

        @pl.when(core.d == 1)
        def _():
            for q in range(SLOTS):
                for c in far(q, low_rim if q < 4 else rim):
                    act(c)

    each(lambda c: c.start())
    n = plan(place, mine, prev, offs, cols, srcs)
    blank(obj)
    start.wait()

    def work(G):
        step = Step(G, n, (offs, cols, srcs), obj, hist, H, tab, acc)

        def ahead(s, _):
            core.arrive(s, my_own, rim, obj)
            step.forward(s)
            return 0

        lax.fori_loop(0, GROUP - 1, ahead, 0)
        core.arrive(GROUP - 1, my_own, rim, obj)
        each(lambda c: c.wait())
        step.detector(inten)

        def back(k, _):
            s = GROUP - 1 - k
            clear(acc, s)
            step.backward(s)
            core.send(s, out_own, out_rim, acc)
            return 0

        lax.fori_loop(0, GROUP, back, 0)

    sized(n, work)
    end = pltpu.make_async_copy(hist.at[GROUP], err, more.at[1])
    end.start()
    core.gone(out_own, out_rim, acc)
    end.wait()


def third_kernel(
    place, mine, prev, my_own, other_own, rim, psi, err, probe, H, tab,
    out_own, out_rim,
    obj, acc, hist, offs, cols, srcs, sem, more,
):
    core = Core(place, sem)

    def load(s):
        return pltpu.make_async_copy(psi.at[s - 1], hist.at[s], more.at[s])

    start = pltpu.make_async_copy(err, hist.at[GROUP], more.at[0])
    start.start()
    load(GROUP - 1).start()
    core.fetch(0, my_own, other_own, rim, obj, True)
    for s in range(GROUP - 2, 0, -1):
        load(s).start()
    n = plan(place, mine, prev, offs, cols, srcs)
    blank(obj)
    start.wait()

    def work(G):
        step = Step(G, n, (offs, cols, srcs), obj, hist, H, tab, acc)
        hist[0, :G * W, :] = jnp.concatenate([jnp.concatenate([probe[0], probe[1]], 1)] * G, 0)

        def back(k, _):
            s = GROUP - 1 - k
            clear(acc, s)
            load(s).wait()
            core.arrive(s, my_own, rim, obj)
            step.backward(s)
            core.send(s, out_own, out_rim, acc)
            return 0

        lax.fori_loop(0, GROUP - 1, back, 0)
        core.arrive(0, my_own, rim, obj)
        clear(acc, 0)
        for j in range(G):
            step.scatter(0, j)
        core.send(0, out_own, out_rim, acc)

    sized(n, work)
    core.gone(out_own, out_rim, acc)


def both_ways(value, outward):
    count = lax.axis_size("tile")
    up = [(i, i - 1) for i in range(1, count)]
    down = [(i, i + 1) for i in range(count - 1)]
    first, second = (down, up) if outward else (up, down)
    pairs = first + [(count + a, count + b) for a, b in second]
    return lax.ppermute(value, ("depth", "tile"), pairs)


def partner(value):
    return lax.ppermute(value, "depth", [(0, 1), (1, 0)])


def packed(depth, above, below, ints):
    side = ints.reshape(4, 4, 2, INTS, W).transpose(1, 2, 3, 0, 4).reshape(4, 2, INTS, 4 * W)
    return jnp.where(
        depth == 0, above[:, :, :RIM], jnp.concatenate([side, below[:, :, RIM:]], axis=2)
    )


def local(
    specimen_layers,
    illumination_field,
    propagator_spectral_angle,
    recorded_intensities,
    patch_upper_edges,
    patch_left_edges,
    occupied_places_per_band,
):
    depth = lax.axis_index("depth")
    tile = lax.axis_index("tile")
    columns = specimen_layers.shape[3]
    count = lax.axis_size("tile")
    place = jnp.stack([depth, tile, jnp.int32(count - 1)]).astype(jnp.int32)
    mine = jnp.concatenate([patch_upper_edges, patch_left_edges, occupied_places_per_band])
    other = partner(specimen_layers)
    prev = lax.ppermute(
        mine, ("depth", "tile"), [(count + i, count + i + 1) for i in range(count - 1)]
    )
    low = packed(depth, specimen_layers, other, recorded_intensities[:4])
    high = packed(depth, other, specimen_layers, recorded_intensities[4:])
    low_rim = both_ways(low, False)
    high_rim = both_ways(high, False)
    H = jnp.stack([jnp.cos(propagator_spectral_angle), jnp.sin(propagator_spectral_angle)])
    tab = jnp.asarray(tables())
    hbm = pl.BlockSpec(memory_space=pl.ANY)
    vm = pl.BlockSpec(memory_space=pltpu.VMEM)
    sm = pl.BlockSpec(memory_space=pltpu.SMEM)
    own = jax.ShapeDtypeStruct((GROUP, 2, W, columns), jnp.float32)
    rim = jax.ShapeDtypeStruct((GROUP, 2, RIM, columns), jnp.float32)
    errors = jax.ShapeDtypeStruct((SLOTS * W, 2 * W), jnp.float32)
    field = pltpu.VMEM((GROUP, 2, BLOCKS, TALL, W), jnp.float32)
    hist = pltpu.VMEM((GROUP + 1, SLOTS * W, 2 * W), jnp.float32)
    tail = [pltpu.SMEM((SLOTS,), jnp.int32)] * 3 + [
        pltpu.SemaphoreType.DMA((GROUP, 2 * BLOCKS)),
        pltpu.SemaphoreType.DMA((GROUP,)),
    ]
    params = pltpu.CompilerParams(vmem_limit_bytes=48 * 1024 * 1024)
    where = (place, mine, prev, specimen_layers, other)
    psi = pl.pallas_call(
        first_kernel,
        out_shape=jax.ShapeDtypeStruct((GROUP, SLOTS * W, 2 * W), jnp.float32),
        in_specs=[sm] * 3 + [hbm] * 3 + [vm] * 3,
        out_specs=hbm,
        scratch_shapes=[field, hist] + tail,
        compiler_params=params,
        name="first",
    )(*where, low_rim, illumination_field, H, tab)
    own_high, rim_high, err = pl.pallas_call(
        second_kernel,
        out_shape=[own, rim, errors],
        in_specs=[sm] * 3 + [hbm] * 6 + [vm] * 2,
        out_specs=[hbm] * 3,
        scratch_shapes=[field, field, hist, pltpu.VMEM((SLOTS, 8, INTS, W), jnp.float32)]
        + tail + [pltpu.SemaphoreType.DMA((72,))],
        compiler_params=params,
        name="second",
    )(
        *where, high_rim, low_rim, psi,
        recorded_intensities.reshape(SLOTS, 8, INTS, W), H, tab,
    )
    came_high = both_ways(rim_high, True)
    own_low, rim_low = pl.pallas_call(
        third_kernel,
        out_shape=[own, rim],
        in_specs=[sm] * 3 + [hbm] * 5 + [vm] * 3,
        out_specs=[hbm] * 2,
        scratch_shapes=[field, field, hist] + tail,
        compiler_params=params,
        name="third",
    )(*where, low_rim, psi, err, illumination_field, H, tab)
    came_low = both_ways(rim_low, True)
    head = jnp.concatenate([came_high, jnp.zeros((GROUP, 2, W - RIM, columns))], axis=2)
    given = jnp.where(depth == 0, own_high + head, own_low)
    taken = partner(given)
    foot = jnp.concatenate([jnp.zeros((GROUP, 2, RIM, columns)), came_high[:, :, INTS:]], axis=2)
    total = jnp.where(depth == 0, own_low, own_high + foot) + taken
    total = lax.optimization_barrier(total)
    crossed = lax.ppermute(came_low, "depth", [(1, 0)])
    late = jnp.concatenate([came_low, crossed[:, :, INTS:]], axis=2)
    return total + jnp.where(depth == 0, late, 0.0)


def solution(mesh):
    placed = (
        P("depth", None, "tile", None),
        P(),
        P(),
        P("tile", None, None),
        P("tile"),
        P("tile"),
        P("tile"),
    )
    return jax.shard_map(
        local, mesh=mesh, in_specs=placed, out_specs=P("depth", None, "tile", None), check_vma=False
    )
```

profile of v0, /device:TPU:2, one launch (start us, length us, event | category | flops | bytes accessed | tf_op | source)
XLA Modules:
  0.0 109.5 jit_solution(12614501269891153105)
XLA Ops:
  0.0 2.2 %slice.29 = f32[4,2,56,512]{3,2,1,0:T(8,128)} slice(f32[4,2,128,512]{3,2,1,0:T(8,128)} %my_own.5), slice={[0:4], [0:2], [72:128], [0:512]} | slice | bytes 1835008 | tf_op jit(solution)/shard_map/slice | solution.py:437
  2.3 0.2 copy.13
  2.5 0.8 reshape.18
  3.3 0.2 copy.14
  3.5 0.1 reshape.16
  3.6 0.9 collective-permute-done.1.other_own
  4.5 1.2 %slice.32 = f32[4,2,56,512]{3,2,1,0:T(8,128)S(1)} slice(f32[4,2,128,512]{3,2,1,0:T(8,128)} %collective-permute-done.1.other_own), slice={[0:4], [0:2], [72:128], [0:512]} | slice | bytes 1835008 | tf_op jit(solution)/shard_map/slice | solution.py:437
  5.8 1.3 %maximum_select_fusion.1 = f32[4,2,72,512]{3,2,1,0:T(8,128)} fusion(f32[4,2,56,512]{3,2,1,0:T(8,128)S(1)} %slice.32, f32[4,2,16,512]{3,2,1,0:T(8,128)S(1)} %reshape.16, f32[4,2,128,512]{3,2,1,0:T(8,128)S(1)} %copy-done, pred[]{:T(512)S(6)} %eq.2), kind=kLoop, calls=%fused_computation.5 | loop fusion | flops 589824 | bytes 3538945 | tf_op jit(solution)/shard_map/jit(_where)/select_n | solution.py:436
  7.0 8.5 %collective-permute-start.2 = (f32[4,2,72,512]{3,2,1,0:T(8,128)}, f32[4,2,72,512]{3,2,1,0:T(8,128)S(1)}, u32[]{:S(2)}, u32[]{:S(2)}) collective-permute-start(f32[4,2,72,512]{3,2,1,0:T(8,128)} %maximum_select_fusion.1), channel_id=1, source_target_pairs={{1,0},{2,1},{3,2},{4,3},{5,4},{6,5},{7,6},{8,7},{9,8},{10,9},{11,1... | collective-permute-start | bytes 3538952 | tf_op jit(solution)/shard_map/ppermute | solution.py:427
  15.6 2.5 %slice_select_fusion = f32[4,2,72,512]{3,2,1,0:T(8,128)} fusion(f32[4,2,128,512]{3,2,1,0:T(8,128)} %collective-permute-done.1.other_own, f32[4,2,56,512]{3,2,1,0:T(8,128)S(1)} %copy-done.9, f32[4,2,16,512]{3,2,1,0:T(8,128)S(1)} %copy-done.10, pred[]{:T(512)S(6)} %eq.2), kind=kLoop, calls=%fused_computation.4 | loop fusion | flops 589824 | bytes 3538945 | tf_op jit(solution)/shard_map/jit(_where)/select_n | solution.py:436
  18.1 2.3 %collective-permute-start.3 = (f32[4,2,72,512]{3,2,1,0:T(8,128)}, f32[4,2,72,512]{3,2,1,0:T(8,128)}, u32[]{:S(2)}, u32[]{:S(2)}) collective-permute-start(f32[4,2,72,512]{3,2,1,0:T(8,128)} %slice_select_fusion), channel_id=1, source_target_pairs={{1,0},{2,1},{3,2},{4,3},{5,4},{6,5},{7,6},{8,7},{9,8},{10,9},{11,1... | collective-permute-start | bytes 3538952 | tf_op jit(solution)/shard_map/ppermute | solution.py:427
  21.1 0.1 pad_add_fusion.1.mine
  21.1 0.7 collective-permute-start
  21.8 0.2 cosine_bitcast_fusion
  22.1 0.1 pad_add_fusion.place
  22.2 7.4 %collective-permute-done.2.rim.low_rim = f32[4,2,72,512]{3,2,1,0:T(8,128)S(1)} collective-permute-done((f32[4,2,72,512]{3,2,1,0:T(8,128)}, f32[4,2,72,512]{3,2,1,0:T(8,128)S(1)}, u32[]{:S(2)}, u32[]{:S(2)}) %collective-permute-start.2) | collective-permute-done | bytes 1179680 | tf_op jit(solution)/shard_map/ppermute | solution.py:427
  29.6 1.0 copy-done.1
  30.6 9.8 %first.1.psi = f32[4,1024,256]{2,1,0:T(8,128)} custom-call(s32[3]{0:T(128)S(1)} %pad_add_fusion.place, s32[17]{0:T(128)S(1)} %pad_add_fusion.1.mine, s32[17]{0:T(128)S(1)} %collective-permute-done.prev, f32[4,2,128,512]{3,2,1,0:T(8,128)S(1)} %copy-done, f32[4,2,128,512]{3,2,1,0:T(8,128)} %collective-permute-done.1.other_own, ...), custom_call_target="tpu_custom_call" | custom-call | tf_op jit(solution)/shard_map/first/pallas_call | solution.py:480
  40.5 1.8 %collective-permute-done.3.rim = f32[4,2,72,512]{3,2,1,0:T(8,128)} collective-permute-done((f32[4,2,72,512]{3,2,1,0:T(8,128)}, f32[4,2,72,512]{3,2,1,0:T(8,128)}, u32[]{:S(2)}, u32[]{:S(2)}) %collective-permute-start.3) | collective-permute-done | bytes 1179680 | tf_op jit(solution)/shard_map/ppermute | solution.py:427
  42.2 19.7 %second.1 = (f32[4,2,128,512]{3,2,1,0:T(8,128)}, f32[4,2,72,512]{3,2,1,0:T(8,128)S(1)}, f32[1024,256]{1,0:T(8,128)S(1)}) custom-call(s32[3]{0:T(128)S(1)} %pad_add_fusion.place, s32[17]{0:T(128)S(1)} %pad_add_fusion.1.mine, s32[17]{0:T(128)S(1)} %collective-permute-done.prev, f32[4,2,128,512]{3,2,1,0:T(8,128)} %my_own.5, ...), custom_call_target="tpu_custom_call" | custom-call | tf_op jit(solution)/shard_map/second/pallas_call | solution.py:489
  61.9 1.9 %collective-permute-start.4 = (f32[4,2,72,512]{3,2,1,0:T(8,128)S(1)}, f32[4,2,72,512]{3,2,1,0:T(8,128)S(1)}, u32[]{:S(2)}, u32[]{:S(2)}) collective-permute-start(f32[4,2,72,512]{3,2,1,0:T(8,128)S(1)} %get-tuple-element.13), channel_id=1, source_target_pairs={{0,1},{1,2},{2,3},{3,4},{4,5},{5,6},{6,7},{7,8},{8,9},{9,10},{10,1... | collective-permute-start | bytes 3538952 | tf_op jit(solution)/shard_map/ppermute | solution.py:427
  63.8 9.9 %third.1 = (f32[4,2,128,512]{3,2,1,0:T(8,128)}, f32[4,2,72,512]{3,2,1,0:T(8,128)S(1)}) custom-call(s32[3]{0:T(128)S(1)} %pad_add_fusion.place, s32[17]{0:T(128)S(1)} %pad_add_fusion.1.mine, s32[17]{0:T(128)S(1)} %collective-permute-done.prev, f32[4,2,128,512]{3,2,1,0:T(8,128)} %my_own.5, f32[4,2,128,512]{3,2,1,0:T(8,128)} %collective-permute-done.1.other_own, ...), custom_call_target="tpu_custom_call" | custom-call | tf_op jit(solution)/shard_map/third/pallas_call | solution.py:503
  73.7 2.1 %collective-permute-start.6 = (f32[4,2,72,512]{3,2,1,0:T(8,128)S(1)}, f32[4,2,72,512]{3,2,1,0:T(8,128)S(1)}, u32[]{:S(2)}, u32[]{:S(2)}) collective-permute-start(f32[4,2,72,512]{3,2,1,0:T(8,128)S(1)} %get-tuple-element.14), channel_id=1, source_target_pairs={{0,1},{1,2},{2,3},{3,4},{4,5},{5,6},{6,7},{7,8},{8,9},{9,10},{10,1... | collective-permute-start | bytes 3538952 | tf_op jit(solution)/shard_map/ppermute | solution.py:427
  75.9 8.6 %collective-permute-done.4 = f32[4,2,72,512]{3,2,1,0:T(8,128)S(1)} collective-permute-done((f32[4,2,72,512]{3,2,1,0:T(8,128)S(1)}, f32[4,2,72,512]{3,2,1,0:T(8,128)S(1)}, u32[]{:S(2)}, u32[]{:S(2)}) %collective-permute-start.4) | collective-permute-done | bytes 1179680 | tf_op jit(solution)/shard_map/ppermute | solution.py:427
  84.5 0.7 add_select_fusion
  85.2 7.5 %collective-permute-start.5 = (f32[4,2,128,512]{3,2,1,0:T(8,128)S(1)}, f32[4,2,128,512]{3,2,1,0:T(8,128)S(1)}, u32[]{:S(2)}, u32[]{:S(2)}) collective-permute-start(f32[4,2,128,512]{3,2,1,0:T(8,128)S(1)} %add_select_fusion), channel_id=1, source_target_pairs={{0,64},{64,0},{1,65},{65,1},{2,66},{66,2},{3,67},{67,3},{4,68},{68... | collective-permute-start | bytes 6291464 | tf_op jit(solution)/shard_map/ppermute | solution.py:431
  92.7 4.5 %collective-permute-done.6 = f32[4,2,72,512]{3,2,1,0:T(8,128)S(1)} collective-permute-done((f32[4,2,72,512]{3,2,1,0:T(8,128)S(1)}, f32[4,2,72,512]{3,2,1,0:T(8,128)S(1)}, u32[]{:S(2)}, u32[]{:S(2)}) %collective-permute-start.6) | collective-permute-done | bytes 1179680 | tf_op jit(solution)/shard_map/ppermute | solution.py:427
  97.2 1.3 %collective-permute-start.7 = (f32[4,2,72,512]{3,2,1,0:T(8,128)S(1)}, f32[4,2,72,512]{3,2,1,0:T(8,128)S(1)}, u32[]{:S(2)}, u32[]{:S(2)}) collective-permute-start(f32[4,2,72,512]{3,2,1,0:T(8,128)S(1)} %collective-permute-done.6), channel_id=1, source_target_pairs={{64,0},{65,1},{66,2},{67,3},{68,4},{69,5},{70,6},{71,7},{72,8},{73... | collective-permute-start | bytes 3538952 | tf_op jit(solution)/shard_map/ppermute | solution.py:519
  98.5 8.2 %collective-permute-done.7 = f32[4,2,72,512]{3,2,1,0:T(8,128)S(1)} collective-permute-done((f32[4,2,72,512]{3,2,1,0:T(8,128)S(1)}, f32[4,2,72,512]{3,2,1,0:T(8,128)S(1)}, u32[]{:S(2)}, u32[]{:S(2)}) %collective-permute-start.7) | collective-permute-done | bytes 1179680 | tf_op jit(solution)/shard_map/ppermute | solution.py:519
  106.7 0.1 slice.35
  106.8 0.9 select_add_fusion
  107.7 1.8 %fusion = f32[4,2,128,512]{3,2,1,0:T(8,128)} fusion(f32[4,2,128,512]{3,2,1,0:T(8,128)S(1)} %select_add_fusion, f32[4,2,56,512]{3,2,1,0:T(8,128)S(1)} %slice.35, f32[4,2,72,512]{3,2,1,0:T(8,128)S(1)} %collective-permute-done.6, pred[]{:T(512)S(6)} %eq.2), kind=kLoop, calls=%fused_computation.1 | loop fusion | flops 1572864 | bytes 6291457 | tf_op jit(solution)/shard_map/add | solution.py:521
  (34 shorter events, 0.1 us)
Async XLA Ops:
  0.0 2.2 %copy-start.3 = (f32[8,128,128]{2,1,0:T(8,128)S(1)}, f32[8,128,128]{2,1,0:T(8,128)}, u32[]{:S(2)}) copy-start(f32[8,128,128]{2,1,0:T(8,128)} %param.11) | copy-start | bytes 1572868
  0.0 4.5 %collective-permute-start.1 = (f32[4,2,128,512]{3,2,1,0:T(8,128)}, f32[4,2,128,512]{3,2,1,0:T(8,128)}, u32[]{:S(2)}, u32[]{:S(2)}) collective-permute-start(f32[4,2,128,512]{3,2,1,0:T(8,128)} %my_own.5), channel_id=1, source_target_pairs={{0,64},{64,0},{1,65},{65,1},{2,66},{66,2},{3,67},{67,3},{4,68},{68... | collective-permute-start | bytes 6291464 | tf_op jit(solution)/shard_map/ppermute | solution.py:431
  2.3 3.5 %copy-start = (f32[4,2,128,512]{3,2,1,0:T(8,128)S(1)}, f32[4,2,128,512]{3,2,1,0:T(8,128)}, u32[]{:S(2)}) copy-start(f32[4,2,128,512]{3,2,1,0:T(8,128)} %my_own.5) | copy-start | bytes 6291460
  5.8 9.8 %copy-start.9 = (f32[4,2,56,512]{3,2,1,0:T(8,128)S(1)}, f32[4,2,56,512]{3,2,1,0:T(8,128)}, u32[]{:S(2)}) copy-start(f32[4,2,56,512]{3,2,1,0:T(8,128)} %slice.29) | copy-start | bytes 2752516
  5.8 9.8 %copy-start.10 = (f32[4,2,16,512]{3,2,1,0:T(8,128)S(1)}, f32[4,2,16,512]{3,2,1,0:T(8,128)}, u32[]{:S(2)}) copy-start(f32[4,2,16,512]{3,2,1,0:T(8,128)} %reshape.18) | copy-start | bytes 786436
  7.0 14.0 %copy-start.12 = (s32[8]{0:T(128)S(1)}, s32[8]{0:T(128)}, u32[]{:S(2)}) copy-start(s32[8]{0:T(128)} %param.13) | copy-start | bytes 100
  7.0 14.0 %copy-start.13 = (s32[8]{0:T(128)S(1)}, s32[8]{0:T(128)}, u32[]{:S(2)}) copy-start(s32[8]{0:T(128)} %param.12) | copy-start | bytes 100
  7.0 14.8 %copy-start.11 = (f32[128,128]{1,0:T(8,128)S(1)}, f32[128,128]{1,0:T(8,128)}, u32[]{:S(2)}) copy-start(f32[128,128]{1,0:T(8,128)} %param.10) | copy-start | bytes 196612
  7.0 22.5 %copy-start.5 = (f32[2,128,128]{2,1,0:T(8,128)S(1)}, f32[2,128,128]{2,1,0:T(8,128)}, u32[]{:S(2)}) copy-start(f32[2,128,128]{2,1,0:T(8,128)} %probe.3) | copy-start | bytes 393220
  7.0 22.5 %collective-permute-start.2 = (f32[4,2,72,512]{3,2,1,0:T(8,128)}, f32[4,2,72,512]{3,2,1,0:T(8,128)S(1)}, u32[]{:S(2)}, u32[]{:S(2)}) collective-permute-start(f32[4,2,72,512]{3,2,1,0:T(8,128)} %maximum_select_fusion.1), channel_id=1, source_target_pairs={{1,0},{2,1},{3,2},{4,3},{5,4},{6,5},{7,6},{8,7},{9,8},{10,9},{11,1... | collective-permute-start | bytes 3538952 | tf_op jit(solution)/shard_map/ppermute | solution.py:427
  18.1 24.1 %collective-permute-start.3 = (f32[4,2,72,512]{3,2,1,0:T(8,128)}, f32[4,2,72,512]{3,2,1,0:T(8,128)}, u32[]{:S(2)}, u32[]{:S(2)}) collective-permute-start(f32[4,2,72,512]{3,2,1,0:T(8,128)} %slice_select_fusion), channel_id=1, source_target_pairs={{1,0},{2,1},{3,2},{4,3},{5,4},{6,5},{7,6},{8,7},{9,8},{10,9},{11,1... | collective-permute-start | bytes 3538952 | tf_op jit(solution)/shard_map/ppermute | solution.py:427
  21.1 1.0 collective-permute-start
  29.6 1.0 copy-start.1
  30.6 11.6 %copy-start.2 = (bf16[2,2,256,256]{3,2,1,0:T(8,128)(2,1)S(1)}, bf16[2,2,256,256]{3,2,1,0:T(8,128)(2,1)}, u32[]{:S(2)}) copy-start(bf16[2,2,256,256]{3,2,1,0:T(8,128)(2,1)} %constant.19.clone.tab) | copy-start | bytes 1572868
  30.6 11.6 %copy-start.4 = (f32[8,128,128]{2,1,0:T(8,128)S(1)}, f32[8,128,128]{2,1,0:T(8,128)}, u32[]{:S(2)}) copy-start(f32[8,128,128]{2,1,0:T(8,128)} %param.11) | copy-start | bytes 1572868
  61.9 22.7 %collective-permute-start.4 = (f32[4,2,72,512]{3,2,1,0:T(8,128)S(1)}, f32[4,2,72,512]{3,2,1,0:T(8,128)S(1)}, u32[]{:S(2)}, u32[]{:S(2)}) collective-permute-start(f32[4,2,72,512]{3,2,1,0:T(8,128)S(1)} %get-tuple-element.13), channel_id=1, source_target_pairs={{0,1},{1,2},{2,3},{3,4},{4,5},{5,6},{6,7},{7,8},{8,9},{9,10},{10,1... | collective-permute-start | bytes 3538952 | tf_op jit(solution)/shard_map/ppermute | solution.py:427
  63.8 20.7 %copy-start.6 = (f32[4,2,128,512]{3,2,1,0:T(8,128)S(1)}, f32[4,2,128,512]{3,2,1,0:T(8,128)}, u32[]{:S(2)}) copy-start(f32[4,2,128,512]{3,2,1,0:T(8,128)} %get-tuple-element.12) | copy-start | bytes 6291460
  73.7 23.4 %collective-permute-start.6 = (f32[4,2,72,512]{3,2,1,0:T(8,128)S(1)}, f32[4,2,72,512]{3,2,1,0:T(8,128)S(1)}, u32[]{:S(2)}, u32[]{:S(2)}) collective-permute-start(f32[4,2,72,512]{3,2,1,0:T(8,128)S(1)} %get-tuple-element.14), channel_id=1, source_target_pairs={{0,1},{1,2},{2,3},{3,4},{4,5},{5,6},{6,7},{7,8},{8,9},{9,10},{10,1... | collective-permute-start | bytes 3538952 | tf_op jit(solution)/shard_map/ppermute | solution.py:427
  84.5 13.9 %copy-start.8 = (f32[4,2,72,512]{3,2,1,0:T(8,128)}, f32[4,2,72,512]{3,2,1,0:T(8,128)S(1)}, u32[]{:S(2)}) copy-start(f32[4,2,72,512]{3,2,1,0:T(8,128)S(1)} %collective-permute-done.4) | copy-start | bytes 3538948
  85.2 21.6 %copy-start.7 = (f32[4,2,128,512]{3,2,1,0:T(8,128)S(1)}, f32[4,2,128,512]{3,2,1,0:T(8,128)}, u32[]{:S(2)}) copy-start(f32[4,2,128,512]{3,2,1,0:T(8,128)} %get-tuple-element.11) | copy-start | bytes 6291460
  85.2 21.6 %collective-permute-start.5 = (f32[4,2,128,512]{3,2,1,0:T(8,128)S(1)}, f32[4,2,128,512]{3,2,1,0:T(8,128)S(1)}, u32[]{:S(2)}, u32[]{:S(2)}) collective-permute-start(f32[4,2,128,512]{3,2,1,0:T(8,128)S(1)} %add_select_fusion), channel_id=1, source_target_pairs={{0,64},{64,0},{1,65},{65,1},{2,66},{66,2},{3,67},{67,3},{4,68},{68... | collective-permute-start | bytes 6291464 | tf_op jit(solution)/shard_map/ppermute | solution.py:431
  97.2 9.6 %collective-permute-start.7 = (f32[4,2,72,512]{3,2,1,0:T(8,128)S(1)}, f32[4,2,72,512]{3,2,1,0:T(8,128)S(1)}, u32[]{:S(2)}, u32[]{:S(2)}) collective-permute-start(f32[4,2,72,512]{3,2,1,0:T(8,128)S(1)} %collective-permute-done.6), channel_id=1, source_target_pairs={{64,0},{65,1},{66,2},{67,3},{68,4},{69,5},{70,6},{71,7},{72,8},{73... | collective-permute-start | bytes 3538952 | tf_op jit(solution)/shard_map/ppermute | solution.py:519
  98.5 8.3 %slice-start = ((f32[4,2,72,512]{3,2,1,0:T(8,128)}), f32[4,2,56,512]{3,2,1,0:T(8,128)S(1)}, s32[]{:S(2)}) async-start(f32[4,2,72,512]{3,2,1,0:T(8,128)} %copy-done.8), calls=%async_computation | async-start | bytes 1835008 | tf_op jit(solution)/shard_map/slice | solution.py:516
where the time goes:
time: 111 us; the launch traced here: 110 us
  Pallas kernels  39.4 us (35%)
  waiting for transfers between devices  31.4 us (28%)
  starting transfers between devices  24.3 us (22%)
  other arithmetic  7.29 us (7%)
  local copies, waits for them, and re-layouts  6.19 us (6%)
    ppermute x4, waiting for transfers between devices, both_ways(): return lax.ppermute(value, ('depth', 'tile'), pairs)  22.2 us
    pallas_call x1, Pallas kernels, local(): pl.pallas_call(second_kernel, out_shape=[own, rim, errors], in_specs=[sm]...  19.7 us
    ppermute x4, starting transfers between devices, both_ways(): return lax.ppermute(value, ('depth', 'tile'), pairs)  14.9 us
    pallas_call x1, Pallas kernels, local(): pl.pallas_call(third_kernel, out_shape=[own, rim], in_specs=[sm] * 3 + [h...  9.92 us
    pallas_call x1, Pallas kernels, local(): pl.pallas_call(first_kernel, out_shape=jax.ShapeDtypeStruct((GROUP, SLOTS...  9.83 us
    ppermute x1, waiting for transfers between devices, local(): crossed = lax.ppermute(came_low, 'depth', [(1, 0)])  8.25 us
    ppermute x2, starting transfers between devices, partner(): return lax.ppermute(value, 'depth', [(0, 1), (1, 0)])  7.52 us
    select_n x2, other arithmetic, packed(): jnp.where(depth == 0, above[:, :, :RIM], jnp.concatenate([side, below[:,...  3.78 us
  transfers between devices with their start and end apart: 8, of which 6 were waited for; matrix products, arithmetic and copies ran while one was open for 7% of the time, Pallas kernels for 18%

commit v1 on v0

--- a/solution.py
+++ b/solution.py
@@ -228,26 +228,22 @@
                 pairs.append(pltpu.make_async_copy(a, b, self.sem.at[s, 2 * cb + k]))
         return pairs
 
-    def fetch(self, owner, mine, other, rim, obj, downward=False):
+    def fetch(self, owner, mine, other, rims, obj, downward=False):
         def one(i, _):
             s = GROUP - 1 - i if downward else i
-
-            @pl.when(self.d == owner)
-            def _():
-                for c in self.moves(s, mine, rim, obj, False):
-                    c.start()
-
-            @pl.when(self.d != owner)
-            def _():
-                for c in self.moves(s, other, rim, obj, False):
-                    c.start()
+            for d in range(2):
+
+                @pl.when(self.d == d)
+                def _(d=d):
+                    for c in self.moves(s, mine if d == owner else other, rims[d], obj, False):
+                        c.start()
 
             return 0
 
         lax.fori_loop(0, GROUP, one, 0)
 
-    def arrive(self, s, mine, rim, obj):
-        for c in self.moves(s, mine, rim, obj, False):
+    def arrive(self, s, mine, rims, obj):
+        for c in self.moves(s, mine, rims[0], obj, False):
             c.wait()
 
     def send(self, s, own, rim, acc):
@@ -277,11 +273,12 @@
 
 
 def first_kernel(
-    place, mine, prev, my_own, other_own, rim, probe, H, tab, psi,
+    place, mine, prev, my_own, other_own, rim_a, rim_b, probe, H, tab, psi,
     obj, hist, offs, cols, srcs, sem, more,
 ):
     core = Core(place, sem)
-    core.fetch(0, my_own, other_own, rim, obj)
+    rims = (rim_a, rim_b)
+    core.fetch(0, my_own, other_own, rims, obj)
     n = plan(place, mine, prev, offs, cols, srcs)
     blank(obj)
 
@@ -293,7 +290,7 @@
         hist[0, :G * W, :] = jnp.concatenate([jnp.concatenate([probe[0], probe[1]], 1)] * G, 0)
 
         def ahead(s, _):
-            core.arrive(s, my_own, rim, obj)
+            core.arrive(s, my_own, rims, obj)
             step.forward(s)
             save(s).start()
             return 0
@@ -306,14 +303,15 @@
 
 
 def second_kernel(
-    place, mine, prev, my_own, other_own, rim, low_rim, psi, ints, H, tab,
+    place, mine, prev, my_own, other_own, rim_a, rim_b, low_b, psi, ints, H, tab,
     out_own, out_rim, err,
     obj, acc, hist, inten, offs, cols, srcs, sem, more, isem,
 ):
     core = Core(place, sem)
+    rims = (rim_a, rim_b)
     start = pltpu.make_async_copy(psi.at[GROUP - 1], hist.at[0], more.at[0])
     start.start()
-    core.fetch(1, my_own, other_own, rim, obj)
+    core.fetch(1, my_own, other_own, rims, obj)
 
     def near(q):
         return pltpu.make_async_copy(ints.at[q], inten.at[q], isem.at[q])
@@ -337,7 +335,7 @@
         @pl.when(core.d == 1)
         def _():
             for q in range(SLOTS):
-                for c in far(q, low_rim if q < 4 else rim):
+                for c in far(q, low_b if q < 4 else rim_b):
                     act(c)
 
     each(lambda c: c.start())
@@ -349,12 +347,12 @@
         step = Step(G, n, (offs, cols, srcs), obj, hist, H, tab, acc)
 
         def ahead(s, _):
-            core.arrive(s, my_own, rim, obj)
+            core.arrive(s, my_own, rims, obj)
             step.forward(s)
             return 0
 
         lax.fori_loop(0, GROUP - 1, ahead, 0)
-        core.arrive(GROUP - 1, my_own, rim, obj)
+        core.arrive(GROUP - 1, my_own, rims, obj)
         each(lambda c: c.wait())
         step.detector(inten)
 
@@ -375,11 +373,12 @@
 
 
 def third_kernel(
-    place, mine, prev, my_own, other_own, rim, psi, err, probe, H, tab,
+    place, mine, prev, my_own, other_own, rim_a, rim_b, psi, err, probe, H, tab,
     out_own, out_rim,
     obj, acc, hist, offs, cols, srcs, sem, more,
 ):
     core = Core(place, sem)
+    rims = (rim_a, rim_b)
 
     def load(s):
         return pltpu.make_async_copy(psi.at[s - 1], hist.at[s], more.at[s])
@@ -387,7 +386,7 @@
     start = pltpu.make_async_copy(err, hist.at[GROUP], more.at[0])
     start.start()
     load(GROUP - 1).start()
-    core.fetch(0, my_own, other_own, rim, obj, True)
+    core.fetch(0, my_own, other_own, rims, obj, True)
     for s in range(GROUP - 2, 0, -1):
         load(s).start()
     n = plan(place, mine, prev, offs, cols, srcs)
@@ -402,13 +401,13 @@
             s = GROUP - 1 - k
             clear(acc, s)
             load(s).wait()
-            core.arrive(s, my_own, rim, obj)
+            core.arrive(s, my_own, rims, obj)
             step.backward(s)
             core.send(s, out_own, out_rim, acc)
             return 0
 
         lax.fori_loop(0, GROUP - 1, back, 0)
-        core.arrive(0, my_own, rim, obj)
+        core.arrive(0, my_own, rims, obj)
         clear(acc, 0)
         for j in range(G):
             step.scatter(0, j)
@@ -418,12 +417,10 @@
     core.gone(out_own, out_rim, acc)
 
 
-def both_ways(value, outward):
+def outward(value):
     count = lax.axis_size("tile")
-    up = [(i, i - 1) for i in range(1, count)]
-    down = [(i, i + 1) for i in range(count - 1)]
-    first, second = (down, up) if outward else (up, down)
-    pairs = first + [(count + a, count + b) for a, b in second]
+    pairs = [(i, i + 1) for i in range(count - 1)]
+    pairs += [(count + i, count + i - 1) for i in range(1, count)]
     return lax.ppermute(value, ("depth", "tile"), pairs)
 
 
@@ -431,11 +428,11 @@
     return lax.ppermute(value, "depth", [(0, 1), (1, 0)])
 
 
-def packed(depth, above, below, ints):
-    side = ints.reshape(4, 4, 2, INTS, W).transpose(1, 2, 3, 0, 4).reshape(4, 2, INTS, 4 * W)
-    return jnp.where(
-        depth == 0, above[:, :, :RIM], jnp.concatenate([side, below[:, :, RIM:]], axis=2)
-    )
+def strips(value, by, source, target):
+    count = lax.axis_size("tile")
+    steps = [(i, i + by) for i in range(count) if 0 <= i + by < count]
+    pairs = [(source * count + a, target * count + b) for a, b in steps]
+    return lax.ppermute(value, ("depth", "tile"), pairs)
 
 
 def local(
@@ -454,13 +451,15 @@
     place = jnp.stack([depth, tile, jnp.int32(count - 1)]).astype(jnp.int32)
     mine = jnp.concatenate([patch_upper_edges, patch_left_edges, occupied_places_per_band])
     other = partner(specimen_layers)
-    prev = lax.ppermute(
-        mine, ("depth", "tile"), [(count + i, count + i + 1) for i in range(count - 1)]
-    )
-    low = packed(depth, specimen_layers, other, recorded_intensities[:4])
-    high = packed(depth, other, specimen_layers, recorded_intensities[4:])
-    low_rim = both_ways(low, False)
-    high_rim = both_ways(high, False)
+    prev = strips(mine, 1, 1, 1)
+    ints = jnp.where(depth == 0, recorded_intensities[:4], recorded_intensities[4:])
+    side = ints.reshape(4, 4, 2, INTS, W).transpose(1, 2, 3, 0, 4).reshape(4, 2, INTS, columns)
+    top = specimen_layers[:, :, :RIM]
+    bottom = jnp.concatenate([side, specimen_layers[:, :, RIM:]], axis=2)
+    low_a = strips(top, -1, 0, 0)
+    low_b = strips(bottom, 1, 0, 1)
+    high_a = strips(top, -1, 1, 0)
+    high_b = strips(bottom, 1, 1, 1)
     H = jnp.stack([jnp.cos(propagator_spectral_angle), jnp.sin(propagator_spectral_angle)])
     tab = jnp.asarray(tables())
     hbm = pl.BlockSpec(memory_space=pl.ANY)
@@ -480,45 +479,44 @@
     psi = pl.pallas_call(
         first_kernel,
         out_shape=jax.ShapeDtypeStruct((GROUP, SLOTS * W, 2 * W), jnp.float32),
-        in_specs=[sm] * 3 + [hbm] * 3 + [vm] * 3,
+        in_specs=[sm] * 3 + [hbm] * 4 + [vm] * 3,
         out_specs=hbm,
         scratch_shapes=[field, hist] + tail,
         compiler_params=params,
         name="first",
-    )(*where, low_rim, illumination_field, H, tab)
+    )(*where, low_a, low_b, illumination_field, H, tab)
     own_high, rim_high, err = pl.pallas_call(
         second_kernel,
         out_shape=[own, rim, errors],
-        in_specs=[sm] * 3 + [hbm] * 6 + [vm] * 2,
+        in_specs=[sm] * 3 + [hbm] * 7 + [vm] * 2,
         out_specs=[hbm] * 3,
         scratch_shapes=[field, field, hist, pltpu.VMEM((SLOTS, 8, INTS, W), jnp.float32)]
         + tail + [pltpu.SemaphoreType.DMA((72,))],
         compiler_params=params,
         name="second",
     )(
-        *where, high_rim, low_rim, psi,
+        *where, high_a, high_b, low_b, psi,
         recorded_intensities.reshape(SLOTS, 8, INTS, W), H, tab,
     )
-    came_high = both_ways(rim_high, True)
+    came_high = outward(rim_high)
     own_low, rim_low = pl.pallas_call(
         third_kernel,
         out_shape=[own, rim],
-        in_specs=[sm] * 3 + [hbm] * 5 + [vm] * 3,
+        in_specs=[sm] * 3 + [hbm] * 6 + [vm] * 3,
         out_specs=[hbm] * 2,
         scratch_shapes=[field, field, hist] + tail,
         compiler_params=params,
         name="third",
-    )(*where, low_rim, psi, err, illumination_field, H, tab)
-    came_low = both_ways(rim_low, True)
+    )(*where, low_a, low_b, psi, err, illumination_field, H, tab)
+    low_head = strips(rim_low, 1, 0, 0)
+    low_foot = strips(rim_low, -1, 1, 0)
     head = jnp.concatenate([came_high, jnp.zeros((GROUP, 2, W - RIM, columns))], axis=2)
     given = jnp.where(depth == 0, own_high + head, own_low)
     taken = partner(given)
     foot = jnp.concatenate([jnp.zeros((GROUP, 2, RIM, columns)), came_high[:, :, INTS:]], axis=2)
     total = jnp.where(depth == 0, own_low, own_high + foot) + taken
     total = lax.optimization_barrier(total)
-    crossed = lax.ppermute(came_low, "depth", [(1, 0)])
-    late = jnp.concatenate([came_low, crossed[:, :, INTS:]], axis=2)
-    return total + jnp.where(depth == 0, late, 0.0)
+    return total + jnp.concatenate([low_head, low_foot[:, :, INTS:]], axis=2)
 
 
 def solution(mesh):

time: 111 us -> 116 us (1.045)
  waiting for transfers between devices: 31.4 us -> 43.9 us
  starting transfers between devices: 24.3 us -> 18.7 us
  other arithmetic: 7.29 us -> 5.98 us
    ppermute x6 -> x8, waiting for transfers between devices: 30.5 us -> 43.9 us  [the longest x7 33.6 us: strips(): return lax.ppermute(value, ('depth', 'tile'), pairs)]
    ppermute x2, starting transfers between devices: 7.52 us -> 0.09 us  [partner(): return lax.ppermute(value, 'depth', [(0, 1), (1, 0)])]
    select_n x2 -> x1, other arithmetic: 3.78 us -> 0.03 us  [local(): jnp.where(depth == 0, recorded_intensities[:4], recorded_intensities[4:])]
    concatenate x0 -> x1, other arithmetic: none -> 2.32 us  [local(): bottom = jnp.concatenate([side, specimen_layers[:, :, RIM:]], axis=2)]
    ppermute x6 -> x8, starting transfers between devices: 16.8 us -> 18.6 us  [the longest x7 16.7 us: strips(): return lax.ppermute(value, ('depth', 'tile'), pairs)]
    slice x4 -> x3, local copies, waits for them, and re-layouts: 3.57 us -> 3.6 us  [the longest x1 2.52 us: local(): top = specimen_layers[:, :, :RIM]]
  transfers between devices with their start and end apart: 8 -> 10, of which waited for: 6 -> 5; matrix products, arithmetic and copies ran while one was open for 7% -> 7% of each run, Pallas kernels for 18% -> 18%
where the time goes in v1:
time: 116 us; the launch traced here: 115 us
  waiting for transfers between devices  43.9 us (38%)
  Pallas kernels  40 us (34%)
  starting transfers between devices  18.7 us (16%)
  other arithmetic  5.98 us (5%)
  local copies, waits for them, and re-layouts  5.59 us (5%)
    ppermute x7, waiting for transfers between devices, strips(): return lax.ppermute(value, ('depth', 'tile'), pairs)  33.6 us
    pallas_call x1, Pallas kernels, local(): pl.pallas_call(second_kernel, out_shape=[own, rim, errors], in_specs=[sm]...  19.7 us
    ppermute x7, starting transfers between devices, strips(): return lax.ppermute(value, ('depth', 'tile'), pairs)  16.7 us
    ppermute x1, waiting for transfers between devices, outward(): return lax.ppermute(value, ('depth', 'tile'), pairs)  10.3 us
    pallas_call x1, Pallas kernels, local(): pl.pallas_call(first_kernel, out_shape=jax.ShapeDtypeStruct((GROUP, SLOTS...  10.3 us
    pallas_call x1, Pallas kernels, local(): pl.pallas_call(third_kernel, out_shape=[own, rim], in_specs=[sm] * 3 + [h...  10 us
    slice x1, local copies, waits for them, and re-layouts, local(): top = specimen_layers[:, :, :RIM]  2.52 us
  transfers between devices with their start and end apart: 10, of which 5 were waited for; matrix products, arithmetic and copies ran while one was open for 7% of the time, Pallas kernels for 18%

profile of v1, /device:TPU:2, one launch (start us, length us, event | category | flops | bytes accessed | tf_op | source)
XLA Modules:
  0.0 115.2 jit_solution(16160906719143077951)
XLA Ops:
  0.0 0.0 collective-permute-start.1
  0.0 2.5 %slice.18 = f32[4,2,72,512]{3,2,1,0:T(8,128)} slice(f32[4,2,128,512]{3,2,1,0:T(8,128)} %my_own.5), slice={[0:4], [0:2], [0:72], [0:512]} | slice | bytes 2359296 | tf_op jit(solution)/shard_map/slice | solution.py:457
  2.5 8.4 %collective-permute-start.2 = (f32[4,2,72,512]{3,2,1,0:T(8,128)}, f32[4,2,72,512]{3,2,1,0:T(8,128)}, u32[]{:S(2)}, u32[]{:S(2)}) collective-permute-start(f32[4,2,72,512]{3,2,1,0:T(8,128)} %slice.18), channel_id=1, source_target_pairs={{1,0},{2,1},{3,2},{4,3},{5,4},{6,5},{7,6},{8,7},{9,8},{10,9},{11,1... | collective-permute-start | bytes 3538952 | tf_op jit(solution)/shard_map/ppermute | solution.py:435
  10.9 1.0 slice.21
  12.0 0.0 copy-start.7
  12.0 0.2 copy.11
  12.2 0.1 reshape.10
  12.3 2.3 %pad_maximum_fusion = f32[4,2,72,512]{3,2,1,0:T(8,128)} fusion(f32[4,2,56,512]{3,2,1,0:T(8,128)} %slice.21, f32[4,2,16,512]{3,2,1,0:T(8,128)S(1)} %reshape.10), kind=kLoop, calls=%fused_computation.3 | loop fusion | flops 294912 | bytes 2359296 | tf_op jit(solution)/shard_map/concatenate | solution.py:458
  14.6 1.4 %collective-permute-start.3 = (f32[4,2,72,512]{3,2,1,0:T(8,128)}, f32[4,2,72,512]{3,2,1,0:T(8,128)S(1)}, u32[]{:S(2)}, u32[]{:S(2)}) collective-permute-start(f32[4,2,72,512]{3,2,1,0:T(8,128)} %pad_maximum_fusion), channel_id=1, source_target_pairs={{0,65},{1,66},{2,67},{3,68},{4,69},{5,70},{6,71},{7,72},{8,73},{9,... | collective-permute-start | bytes 3538952 | tf_op jit(solution)/shard_map/ppermute | solution.py:435
  16.6 0.1 pad_add_fusion.1.mine
  16.7 0.7 collective-permute-start
  17.4 1.3 %collective-permute-start.4 = (f32[4,2,72,512]{3,2,1,0:T(8,128)}, f32[4,2,72,512]{3,2,1,0:T(8,128)}, u32[]{:S(2)}, u32[]{:S(2)}) collective-permute-start(f32[4,2,72,512]{3,2,1,0:T(8,128)} %slice.18), channel_id=1, source_target_pairs={{65,0},{66,1},{67,2},{68,3},{69,4},{70,5},{71,6},{72,7},{73,8},{74... | collective-permute-start | bytes 3538952 | tf_op jit(solution)/shard_map/ppermute | solution.py:435
  18.7 1.7 %collective-permute-start.5 = (f32[4,2,72,512]{3,2,1,0:T(8,128)}, f32[4,2,72,512]{3,2,1,0:T(8,128)}, u32[]{:S(2)}, u32[]{:S(2)}) collective-permute-start(f32[4,2,72,512]{3,2,1,0:T(8,128)} %pad_maximum_fusion), channel_id=1, source_target_pairs={{64,65},{65,66},{66,67},{67,68},{68,69},{69,70},{70,71},{71,72},{7... | collective-permute-start | bytes 3538952 | tf_op jit(solution)/shard_map/ppermute | solution.py:435
  20.4 0.1 pad_add_fusion.place
  20.4 0.2 cosine_bitcast_fusion
  20.7 8.6 %collective-permute-done.2.rim_a = f32[4,2,72,512]{3,2,1,0:T(8,128)} collective-permute-done((f32[4,2,72,512]{3,2,1,0:T(8,128)}, f32[4,2,72,512]{3,2,1,0:T(8,128)}, u32[]{:S(2)}, u32[]{:S(2)}) %collective-permute-start.2) | collective-permute-done | bytes 1179680 | tf_op jit(solution)/shard_map/ppermute | solution.py:435
  29.3 5.7 %collective-permute-done.3.rim_b.low_b = f32[4,2,72,512]{3,2,1,0:T(8,128)S(1)} collective-permute-done((f32[4,2,72,512]{3,2,1,0:T(8,128)}, f32[4,2,72,512]{3,2,1,0:T(8,128)S(1)}, u32[]{:S(2)}, u32[]{:S(2)}) %collective-permute-start.3) | collective-permute-done | bytes 1179680 | tf_op jit(solution)/shard_map/ppermute | solution.py:435
  35.1 1.4 %copy-done.3 = bf16[2,2,256,256]{3,2,1,0:T(8,128)(2,1)S(1)} copy-done((bf16[2,2,256,256]{3,2,1,0:T(8,128)(2,1)S(1)}, bf16[2,2,256,256]{3,2,1,0:T(8,128)(2,1)}, u32[]{:S(2)}) %copy-start.3) | copy-done | bytes 524312
  36.5 10.3 %first.1.psi = f32[4,1024,256]{2,1,0:T(8,128)} custom-call(s32[3]{0:T(128)S(1)} %pad_add_fusion.place, s32[17]{0:T(128)S(1)} %pad_add_fusion.1.mine, s32[17]{0:T(128)S(1)} %collective-permute-done.prev, f32[4,2,128,512]{3,2,1,0:T(8,128)S(1)} %copy-done, f32[4,2,128,512]{3,2,1,0:T(8,128)} %collective-permute-done.1.other_own, ...), custom_call_target="tpu_custom_call" | custom-call | tf_op jit(solution)/shard_map/first/pallas_call | solution.py:479
  46.9 19.7 %second.1 = (f32[4,2,128,512]{3,2,1,0:T(8,128)}, f32[4,2,72,512]{3,2,1,0:T(8,128)S(1)}, f32[1024,256]{1,0:T(8,128)S(1)}) custom-call(s32[3]{0:T(128)S(1)} %pad_add_fusion.place, s32[17]{0:T(128)S(1)} %pad_add_fusion.1.mine, s32[17]{0:T(128)S(1)} %collective-permute-done.prev, f32[4,2,128,512]{3,2,1,0:T(8,128)} %my_own.5, ...), custom_call_target="tpu_custom_call" | custom-call | tf_op jit(solution)/shard_map/second/pallas_call | solution.py:488
  66.5 1.9 %collective-permute-start.6 = (f32[4,2,72,512]{3,2,1,0:T(8,128)S(1)}, f32[4,2,72,512]{3,2,1,0:T(8,128)S(1)}, u32[]{:S(2)}, u32[]{:S(2)}) collective-permute-start(f32[4,2,72,512]{3,2,1,0:T(8,128)S(1)} %get-tuple-element.13), channel_id=1, source_target_pairs={{0,1},{1,2},{2,3},{3,4},{4,5},{5,6},{6,7},{7,8},{8,9},{9,10},{10,1... | collective-permute-start | bytes 3538952 | tf_op jit(solution)/shard_map/ppermute | solution.py:424
  68.5 10.0 %third.1 = (f32[4,2,128,512]{3,2,1,0:T(8,128)}, f32[4,2,72,512]{3,2,1,0:T(8,128)S(1)}) custom-call(s32[3]{0:T(128)S(1)} %pad_add_fusion.place, s32[17]{0:T(128)S(1)} %pad_add_fusion.1.mine, s32[17]{0:T(128)S(1)} %collective-permute-done.prev, f32[4,2,128,512]{3,2,1,0:T(8,128)} %my_own.5, f32[4,2,128,512]{3,2,1,0:T(8,128)} %collective-permute-done.1.other_own, ...), custom_call_target="tpu_custom_call" | custom-call | tf_op jit(solution)/shard_map/third/pallas_call | solution.py:502
  78.5 10.3 %collective-permute-done.6 = f32[4,2,72,512]{3,2,1,0:T(8,128)S(1)} collective-permute-done((f32[4,2,72,512]{3,2,1,0:T(8,128)S(1)}, f32[4,2,72,512]{3,2,1,0:T(8,128)S(1)}, u32[]{:S(2)}, u32[]{:S(2)}) %collective-permute-start.6) | collective-permute-done | bytes 1179680 | tf_op jit(solution)/shard_map/ppermute | solution.py:424
  88.9 0.7 add_select_fusion
  89.5 0.1 collective-permute-start.7
  89.6 1.4 %collective-permute-start.9 = (f32[4,2,72,512]{3,2,1,0:T(8,128)S(1)}, f32[4,2,72,512]{3,2,1,0:T(8,128)S(1)}, u32[]{:S(2)}, u32[]{:S(2)}) collective-permute-start(f32[4,2,72,512]{3,2,1,0:T(8,128)S(1)} %get-tuple-element.14), channel_id=1, source_target_pairs={{65,0},{66,1},{67,2},{68,3},{69,4},{70,5},{71,6},{72,7},{73,8},{74... | collective-permute-start | bytes 3538952 | tf_op jit(solution)/shard_map/ppermute | solution.py:435
  91.0 1.9 %collective-permute-start.8 = (f32[4,2,72,512]{3,2,1,0:T(8,128)S(1)}, f32[4,2,72,512]{3,2,1,0:T(8,128)S(1)}, u32[]{:S(2)}, u32[]{:S(2)}) collective-permute-start(f32[4,2,72,512]{3,2,1,0:T(8,128)S(1)} %get-tuple-element.14), channel_id=1, source_target_pairs={{0,1},{1,2},{2,3},{3,4},{4,5},{5,6},{6,7},{7,8},{8,9},{9,10},{10,1... | collective-permute-start | bytes 3538952 | tf_op jit(solution)/shard_map/ppermute | solution.py:435
  93.0 14.3 %collective-permute-done.9 = f32[4,2,72,512]{3,2,1,0:T(8,128)S(1)} collective-permute-done((f32[4,2,72,512]{3,2,1,0:T(8,128)S(1)}, f32[4,2,72,512]{3,2,1,0:T(8,128)S(1)}, u32[]{:S(2)}, u32[]{:S(2)}) %collective-permute-start.9) | collective-permute-done | bytes 1179680 | tf_op jit(solution)/shard_map/ppermute | solution.py:435
  107.3 0.1 slice.25
  107.4 1.0 select_add_fusion
  108.4 5.0 %collective-permute-done.8 = f32[4,2,72,512]{3,2,1,0:T(8,128)S(1)} collective-permute-done((f32[4,2,72,512]{3,2,1,0:T(8,128)S(1)}, f32[4,2,72,512]{3,2,1,0:T(8,128)S(1)}, u32[]{:S(2)}, u32[]{:S(2)}) %collective-permute-start.8) | collective-permute-done | bytes 1179680 | tf_op jit(solution)/shard_map/ppermute | solution.py:435
  113.4 1.8 %maximum_add_fusion = f32[4,2,128,512]{3,2,1,0:T(8,128)} fusion(f32[4,2,128,512]{3,2,1,0:T(8,128)S(1)} %select_add_fusion, f32[4,2,56,512]{3,2,1,0:T(8,128)S(1)} %slice.25, f32[4,2,72,512]{3,2,1,0:T(8,128)S(1)} %collective-permute-done.8), kind=kLoop, calls=%fused_computation | loop fusion | flops 1048576 | bytes 6291456 | tf_op jit(solution)/shard_map/add | solution.py:519
  (35 shorter events, 0.1 us)
Async XLA Ops:
  0.0 10.9 %copy-start = (f32[4,2,128,512]{3,2,1,0:T(8,128)S(1)}, f32[4,2,128,512]{3,2,1,0:T(8,128)}, u32[]{:S(2)}) copy-start(f32[4,2,128,512]{3,2,1,0:T(8,128)} %my_own.5) | copy-start | bytes 6291460
  0.0 11.9 %copy-start.5 = (f32[8,128,128]{2,1,0:T(8,128)S(1)}, f32[8,128,128]{2,1,0:T(8,128)}, u32[]{:S(2)}) copy-start(f32[8,128,128]{2,1,0:T(8,128)} %param.11) | copy-start | bytes 1572868
  0.0 35.1 %collective-permute-start.1 = (f32[4,2,128,512]{3,2,1,0:T(8,128)}, f32[4,2,128,512]{3,2,1,0:T(8,128)}, u32[]{:S(2)}, u32[]{:S(2)}) collective-permute-start(f32[4,2,128,512]{3,2,1,0:T(8,128)} %my_own.5), channel_id=1, source_target_pairs={{0,64},{64,0},{1,65},{65,1},{2,66},{66,2},{3,67},{67,3},{4,68},{68... | collective-permute-start | bytes 6291464 | tf_op jit(solution)/shard_map/ppermute | solution.py:428
  2.5 26.8 %collective-permute-start.2 = (f32[4,2,72,512]{3,2,1,0:T(8,128)}, f32[4,2,72,512]{3,2,1,0:T(8,128)}, u32[]{:S(2)}, u32[]{:S(2)}) collective-permute-start(f32[4,2,72,512]{3,2,1,0:T(8,128)} %slice.18), channel_id=1, source_target_pairs={{1,0},{2,1},{3,2},{4,3},{5,4},{6,5},{7,6},{8,7},{9,8},{10,9},{11,1... | collective-permute-start | bytes 3538952 | tf_op jit(solution)/shard_map/ppermute | solution.py:435
  11.9 4.7 %copy-start.12 = (s32[8]{0:T(128)S(1)}, s32[8]{0:T(128)}, u32[]{:S(2)}) copy-start(s32[8]{0:T(128)} %param.13) | copy-start | bytes 100
  11.9 4.7 %copy-start.13 = (s32[8]{0:T(128)S(1)}, s32[8]{0:T(128)}, u32[]{:S(2)}) copy-start(s32[8]{0:T(128)} %param.12) | copy-start | bytes 100
  11.9 8.5 %copy-start.11 = (f32[128,128]{1,0:T(8,128)S(1)}, f32[128,128]{1,0:T(8,128)}, u32[]{:S(2)}) copy-start(f32[128,128]{1,0:T(8,128)} %param.10) | copy-start | bytes 196612
  12.0 23.1 %copy-start.7 = (f32[2,128,128]{2,1,0:T(8,128)S(1)}, f32[2,128,128]{2,1,0:T(8,128)}, u32[]{:S(2)}) copy-start(f32[2,128,128]{2,1,0:T(8,128)} %probe.3) | copy-start | bytes 393220
  14.6 20.5 %collective-permute-start.3 = (f32[4,2,72,512]{3,2,1,0:T(8,128)}, f32[4,2,72,512]{3,2,1,0:T(8,128)S(1)}, u32[]{:S(2)}, u32[]{:S(2)}) collective-permute-start(f32[4,2,72,512]{3,2,1,0:T(8,128)} %pad_maximum_fusion), channel_id=1, source_target_pairs={{0,65},{1,66},{2,67},{3,68},{4,69},{5,70},{6,71},{7,72},{8,73},{9,... | collective-permute-start | bytes 3538952 | tf_op jit(solution)/shard_map/ppermute | solution.py:435
  16.7 2.0 %collective-permute-start = (s32[17]{0:T(128)S(1)}, s32[17]{0:T(128)S(1)}, u32[]{:S(2)}, u32[]{:S(2)}) collective-permute-start(s32[17]{0:T(128)S(1)} %pad_add_fusion.1.mine), channel_id=1, source_target_pairs={{64,65},{65,66},{66,67},{67,68},{68,69},{69,70},{70,71},{71,72},{7... | collective-permute-start | bytes 212 | tf_op jit(solution)/shard_map/ppermute | solution.py:435
  17.4 29.4 %collective-permute-start.4 = (f32[4,2,72,512]{3,2,1,0:T(8,128)}, f32[4,2,72,512]{3,2,1,0:T(8,128)}, u32[]{:S(2)}, u32[]{:S(2)}) collective-permute-start(f32[4,2,72,512]{3,2,1,0:T(8,128)} %slice.18), channel_id=1, source_target_pairs={{65,0},{66,1},{67,2},{68,3},{69,4},{70,5},{71,6},{72,7},{73,8},{74... | collective-permute-start | bytes 3538952 | tf_op jit(solution)/shard_map/ppermute | solution.py:435
  18.7 28.1 %collective-permute-start.5 = (f32[4,2,72,512]{3,2,1,0:T(8,128)}, f32[4,2,72,512]{3,2,1,0:T(8,128)}, u32[]{:S(2)}, u32[]{:S(2)}) collective-permute-start(f32[4,2,72,512]{3,2,1,0:T(8,128)} %pad_maximum_fusion), channel_id=1, source_target_pairs={{64,65},{65,66},{66,67},{67,68},{68,69},{69,70},{70,71},{71,72},{7... | collective-permute-start | bytes 3538952 | tf_op jit(solution)/shard_map/ppermute | solution.py:435
  35.1 11.7 %copy-start.1 = (f32[4,2,72,512]{3,2,1,0:T(8,128)}, f32[4,2,72,512]{3,2,1,0:T(8,128)S(1)}, u32[]{:S(2)}) copy-start(f32[4,2,72,512]{3,2,1,0:T(8,128)S(1)} %collective-permute-done.3.rim_b.low_b) | copy-start | bytes 3538948
  35.1 1.4 %copy-start.3 = (bf16[2,2,256,256]{3,2,1,0:T(8,128)(2,1)S(1)}, bf16[2,2,256,256]{3,2,1,0:T(8,128)(2,1)}, u32[]{:S(2)}) copy-start(bf16[2,2,256,256]{3,2,1,0:T(8,128)(2,1)} %constant.18.clone.tab) | copy-start | bytes 1572868
  36.5 10.3 %copy-start.4 = (bf16[2,2,256,256]{3,2,1,0:T(8,128)(2,1)S(1)}, bf16[2,2,256,256]{3,2,1,0:T(8,128)(2,1)}, u32[]{:S(2)}) copy-start(bf16[2,2,256,256]{3,2,1,0:T(8,128)(2,1)} %constant.18.clone.tab) | copy-start | bytes 1572868
  36.5 10.3 %copy-start.6 = (f32[8,128,128]{2,1,0:T(8,128)S(1)}, f32[8,128,128]{2,1,0:T(8,128)}, u32[]{:S(2)}) copy-start(f32[8,128,128]{2,1,0:T(8,128)} %param.11) | copy-start | bytes 1572868
  46.9 21.6 %copy-start.2 = (f32[4,2,72,512]{3,2,1,0:T(8,128)S(1)}, f32[4,2,72,512]{3,2,1,0:T(8,128)}, u32[]{:S(2)}) copy-start(f32[4,2,72,512]{3,2,1,0:T(8,128)} %copy-done.1) | copy-start | bytes 3538948
  66.5 22.3 %collective-permute-start.6 = (f32[4,2,72,512]{3,2,1,0:T(8,128)S(1)}, f32[4,2,72,512]{3,2,1,0:T(8,128)S(1)}, u32[]{:S(2)}, u32[]{:S(2)}) collective-permute-start(f32[4,2,72,512]{3,2,1,0:T(8,128)S(1)} %get-tuple-element.13), channel_id=1, source_target_pairs={{0,1},{1,2},{2,3},{3,4},{4,5},{5,6},{6,7},{7,8},{8,9},{9,10},{10,1... | collective-permute-start | bytes 3538952 | tf_op jit(solution)/shard_map/ppermute | solution.py:424
  68.5 20.4 %copy-start.8 = (f32[4,2,128,512]{3,2,1,0:T(8,128)S(1)}, f32[4,2,128,512]{3,2,1,0:T(8,128)}, u32[]{:S(2)}) copy-start(f32[4,2,128,512]{3,2,1,0:T(8,128)} %get-tuple-element.12) | copy-start | bytes 6291460
  88.8 4.1 %copy-start.10 = (f32[4,2,72,512]{3,2,1,0:T(8,128)}, f32[4,2,72,512]{3,2,1,0:T(8,128)S(1)}, u32[]{:S(2)}) copy-start(f32[4,2,72,512]{3,2,1,0:T(8,128)S(1)} %collective-permute-done.6) | copy-start | bytes 3538948
  89.5 17.8 %copy-start.9 = (f32[4,2,128,512]{3,2,1,0:T(8,128)S(1)}, f32[4,2,128,512]{3,2,1,0:T(8,128)}, u32[]{:S(2)}) copy-start(f32[4,2,128,512]{3,2,1,0:T(8,128)} %get-tuple-element.11) | copy-start | bytes 6291460
  89.5 17.8 %collective-permute-start.7 = (f32[4,2,128,512]{3,2,1,0:T(8,128)S(1)}, f32[4,2,128,512]{3,2,1,0:T(8,128)S(1)}, u32[]{:S(2)}, u32[]{:S(2)}) collective-permute-start(f32[4,2,128,512]{3,2,1,0:T(8,128)S(1)} %add_select_fusion), channel_id=1, source_target_pairs={{0,64},{64,0},{1,65},{65,1},{2,66},{66,2},{3,67},{67,3},{4,68},{68... | collective-permute-start | bytes 6291464 | tf_op jit(solution)/shard_map/ppermute | solution.py:428
  89.6 17.7 %collective-permute-start.9 = (f32[4,2,72,512]{3,2,1,0:T(8,128)S(1)}, f32[4,2,72,512]{3,2,1,0:T(8,128)S(1)}, u32[]{:S(2)}, u32[]{:S(2)}) collective-permute-start(f32[4,2,72,512]{3,2,1,0:T(8,128)S(1)} %get-tuple-element.14), channel_id=1, source_target_pairs={{65,0},{66,1},{67,2},{68,3},{69,4},{70,5},{71,6},{72,7},{73,8},{74... | collective-permute-start | bytes 3538952 | tf_op jit(solution)/shard_map/ppermute | solution.py:435
  91.0 22.3 %collective-permute-start.8 = (f32[4,2,72,512]{3,2,1,0:T(8,128)S(1)}, f32[4,2,72,512]{3,2,1,0:T(8,128)S(1)}, u32[]{:S(2)}, u32[]{:S(2)}) collective-permute-start(f32[4,2,72,512]{3,2,1,0:T(8,128)S(1)} %get-tuple-element.14), channel_id=1, source_target_pairs={{0,1},{1,2},{2,3},{3,4},{4,5},{5,6},{6,7},{7,8},{8,9},{9,10},{10,1... | collective-permute-start | bytes 3538952 | tf_op jit(solution)/shard_map/ppermute | solution.py:435
  93.0 14.4 %slice-start = ((f32[4,2,72,512]{3,2,1,0:T(8,128)}), f32[4,2,56,512]{3,2,1,0:T(8,128)S(1)}, s32[]{:S(2)}) async-start(f32[4,2,72,512]{3,2,1,0:T(8,128)} %copy-done.10), calls=%async_computation | async-start | bytes 1835008 | tf_op jit(solution)/shard_map/slice | solution.py:516

commit v2 on v0

--- a/solution.py
+++ b/solution.py
@@ -429,6 +429,13 @@
 
 def partner(value):
     return lax.ppermute(value, "depth", [(0, 1), (1, 0)])
+
+
+def strips(value, by, source, target):
+    count = lax.axis_size("tile")
+    steps = [(i, i + by) for i in range(count) if 0 <= i + by < count]
+    pairs = [(source * count + a, target * count + b) for a, b in steps]
+    return lax.ppermute(value, ("depth", "tile"), pairs)
 
 
 def packed(depth, above, below, ints):
@@ -454,9 +461,7 @@
     place = jnp.stack([depth, tile, jnp.int32(count - 1)]).astype(jnp.int32)
     mine = jnp.concatenate([patch_upper_edges, patch_left_edges, occupied_places_per_band])
     other = partner(specimen_layers)
-    prev = lax.ppermute(
-        mine, ("depth", "tile"), [(count + i, count + i + 1) for i in range(count - 1)]
-    )
+    prev = strips(mine, 1, 1, 1)
     low = packed(depth, specimen_layers, other, recorded_intensities[:4])
     high = packed(depth, other, specimen_layers, recorded_intensities[4:])
     low_rim = both_ways(low, False)
@@ -509,16 +514,15 @@
         compiler_params=params,
         name="third",
     )(*where, low_rim, psi, err, illumination_field, H, tab)
-    came_low = both_ways(rim_low, True)
+    low_head = strips(rim_low, 1, 0, 0)
+    low_foot = strips(rim_low, -1, 1, 0)
     head = jnp.concatenate([came_high, jnp.zeros((GROUP, 2, W - RIM, columns))], axis=2)
     given = jnp.where(depth == 0, own_high + head, own_low)
     taken = partner(given)
     foot = jnp.concatenate([jnp.zeros((GROUP, 2, RIM, columns)), came_high[:, :, INTS:]], axis=2)
     total = jnp.where(depth == 0, own_low, own_high + foot) + taken
     total = lax.optimization_barrier(total)
-    crossed = lax.ppermute(came_low, "depth", [(1, 0)])
-    late = jnp.concatenate([came_low, crossed[:, :, INTS:]], axis=2)
-    return total + jnp.where(depth == 0, late, 0.0)
+    return total + jnp.concatenate([low_head, low_foot[:, :, INTS:]], axis=2)
 
 
 def solution(mesh):

time: 111 us -> 119 us (1.072)
  waiting for transfers between devices: 31.4 us -> 40.2 us
    ppermute x2 -> x3, waiting for transfers between devices: 8.25 us -> 19.4 us  [strips(): return lax.ppermute(value, ('depth', 'tile'), pairs)]
    ppermute x4 -> x3, waiting for transfers between devices: 22.2 us -> 19.9 us  [both_ways(): return lax.ppermute(value, ('depth', 'tile'), pairs)]
    ppermute x4 -> x3, starting transfers between devices: 14.9 us -> 12.7 us  [both_ways(): return lax.ppermute(value, ('depth', 'tile'), pairs)]
    ppermute x2 -> x3, starting transfers between devices: 1.93 us -> 3.85 us  [strips(): return lax.ppermute(value, ('depth', 'tile'), pairs)]
  transfers between devices with their start and end apart: 8 -> 8, of which waited for: 6 -> 6; matrix products, arithmetic and copies ran while one was open for 7% -> 6% of each run, Pallas kernels for 18% -> 17%
where the time goes in v2:
time: 119 us; the launch traced here: 118 us
  waiting for transfers between devices  40.2 us (34%)
  Pallas kernels  39.4 us (33%)
  starting transfers between devices  23.8 us (20%)
  other arithmetic  7.28 us (6%)
  local copies, waits for them, and re-layouts  6.19 us (5%)
    ppermute x3, waiting for transfers between devices, both_ways(): return lax.ppermute(value, ('depth', 'tile'), pairs)  19.9 us
    pallas_call x1, Pallas kernels, local(): pl.pallas_call(second_kernel, out_shape=[own, rim, errors], in_specs=[sm]...  19.7 us
    ppermute x3, waiting for transfers between devices, strips(): return lax.ppermute(value, ('depth', 'tile'), pairs)  19.4 us
    ppermute x3, starting transfers between devices, both_ways(): return lax.ppermute(value, ('depth', 'tile'), pairs)  12.7 us
    pallas_call x1, Pallas kernels, local(): pl.pallas_call(third_kernel, out_shape=[own, rim], in_specs=[sm] * 3 + [h...  9.92 us
    pallas_call x1, Pallas kernels, local(): pl.pallas_call(first_kernel, out_shape=jax.ShapeDtypeStruct((GROUP, SLOTS...  9.83 us
    ppermute x2, starting transfers between devices, partner(): return lax.ppermute(value, 'depth', [(0, 1), (1, 0)])  7.22 us
    ppermute x3, starting transfers between devices, strips(): return lax.ppermute(value, ('depth', 'tile'), pairs)  3.85 us
  transfers between devices with their start and end apart: 8, of which 6 were waited for; matrix products, arithmetic and copies ran while one was open for 6% of the time, Pallas kernels for 17%

profile of v2, /device:TPU:2, one launch (start us, length us, event | category | flops | bytes accessed | tf_op | source)
XLA Modules:
  0.0 117.8 jit_solution(13403760371397907205)
XLA Ops:
  0.0 2.2 %slice.29 = f32[4,2,56,512]{3,2,1,0:T(8,128)} slice(f32[4,2,128,512]{3,2,1,0:T(8,128)} %my_own.5), slice={[0:4], [0:2], [72:128], [0:512]} | slice | bytes 1835008 | tf_op jit(solution)/shard_map/slice | solution.py:444
  2.3 0.2 copy.13
  2.5 0.8 reshape.18
  3.3 0.2 copy.14
  3.5 0.1 reshape.16
  3.6 0.9 collective-permute-done.1.other_own
  4.5 1.2 %slice.32 = f32[4,2,56,512]{3,2,1,0:T(8,128)S(1)} slice(f32[4,2,128,512]{3,2,1,0:T(8,128)} %collective-permute-done.1.other_own), slice={[0:4], [0:2], [72:128], [0:512]} | slice | bytes 1835008 | tf_op jit(solution)/shard_map/slice | solution.py:444
  5.8 1.3 %maximum_select_fusion = f32[4,2,72,512]{3,2,1,0:T(8,128)} fusion(f32[4,2,56,512]{3,2,1,0:T(8,128)S(1)} %slice.32, f32[4,2,16,512]{3,2,1,0:T(8,128)S(1)} %reshape.16, f32[4,2,128,512]{3,2,1,0:T(8,128)S(1)} %copy-done, pred[]{:T(512)S(6)} %eq.2), kind=kLoop, calls=%fused_computation.4 | loop fusion | flops 589824 | bytes 3538945 | tf_op jit(solution)/shard_map/jit(_where)/select_n | solution.py:443
  7.0 8.5 %collective-permute-start.2 = (f32[4,2,72,512]{3,2,1,0:T(8,128)}, f32[4,2,72,512]{3,2,1,0:T(8,128)S(1)}, u32[]{:S(2)}, u32[]{:S(2)}) collective-permute-start(f32[4,2,72,512]{3,2,1,0:T(8,128)} %maximum_select_fusion), channel_id=1, source_target_pairs={{1,0},{2,1},{3,2},{4,3},{5,4},{6,5},{7,6},{8,7},{9,8},{10,9},{11,1... | collective-permute-start | bytes 3538952 | tf_op jit(solution)/shard_map/ppermute | solution.py:427
  15.6 2.5 %slice_select_fusion = f32[4,2,72,512]{3,2,1,0:T(8,128)} fusion(f32[4,2,128,512]{3,2,1,0:T(8,128)} %collective-permute-done.1.other_own, f32[4,2,56,512]{3,2,1,0:T(8,128)S(1)} %copy-done.9, f32[4,2,16,512]{3,2,1,0:T(8,128)S(1)} %copy-done.10, pred[]{:T(512)S(6)} %eq.2), kind=kLoop, calls=%fused_computation.3 | loop fusion | flops 589824 | bytes 3538945 | tf_op jit(solution)/shard_map/jit(_where)/select_n | solution.py:443
  18.1 2.3 %collective-permute-start.3 = (f32[4,2,72,512]{3,2,1,0:T(8,128)}, f32[4,2,72,512]{3,2,1,0:T(8,128)}, u32[]{:S(2)}, u32[]{:S(2)}) collective-permute-start(f32[4,2,72,512]{3,2,1,0:T(8,128)} %slice_select_fusion), channel_id=1, source_target_pairs={{1,0},{2,1},{3,2},{4,3},{5,4},{6,5},{7,6},{8,7},{9,8},{10,9},{11,1... | collective-permute-start | bytes 3538952 | tf_op jit(solution)/shard_map/ppermute | solution.py:427
  21.1 0.1 pad_add_fusion.1.mine
  21.1 0.7 collective-permute-start
  21.8 0.2 cosine_bitcast_fusion
  22.1 0.1 pad_add_fusion.place
  22.2 7.4 %collective-permute-done.2.rim.low_rim = f32[4,2,72,512]{3,2,1,0:T(8,128)S(1)} collective-permute-done((f32[4,2,72,512]{3,2,1,0:T(8,128)}, f32[4,2,72,512]{3,2,1,0:T(8,128)S(1)}, u32[]{:S(2)}, u32[]{:S(2)}) %collective-permute-start.2) | collective-permute-done | bytes 1179680 | tf_op jit(solution)/shard_map/ppermute | solution.py:427
  29.6 1.0 copy-done.1
  30.6 9.8 %first.1.psi = f32[4,1024,256]{2,1,0:T(8,128)} custom-call(s32[3]{0:T(128)S(1)} %pad_add_fusion.place, s32[17]{0:T(128)S(1)} %pad_add_fusion.1.mine, s32[17]{0:T(128)S(1)} %collective-permute-done.prev, f32[4,2,128,512]{3,2,1,0:T(8,128)S(1)} %copy-done, f32[4,2,128,512]{3,2,1,0:T(8,128)} %collective-permute-done.1.other_own, ...), custom_call_target="tpu_custom_call" | custom-call | tf_op jit(solution)/shard_map/first/pallas_call | solution.py:485
  40.5 1.8 %collective-permute-done.3.rim = f32[4,2,72,512]{3,2,1,0:T(8,128)} collective-permute-done((f32[4,2,72,512]{3,2,1,0:T(8,128)}, f32[4,2,72,512]{3,2,1,0:T(8,128)}, u32[]{:S(2)}, u32[]{:S(2)}) %collective-permute-start.3) | collective-permute-done | bytes 1179680 | tf_op jit(solution)/shard_map/ppermute | solution.py:427
  42.2 19.7 %second.1 = (f32[4,2,128,512]{3,2,1,0:T(8,128)}, f32[4,2,72,512]{3,2,1,0:T(8,128)S(1)}, f32[1024,256]{1,0:T(8,128)S(1)}) custom-call(s32[3]{0:T(128)S(1)} %pad_add_fusion.place, s32[17]{0:T(128)S(1)} %pad_add_fusion.1.mine, s32[17]{0:T(128)S(1)} %collective-permute-done.prev, f32[4,2,128,512]{3,2,1,0:T(8,128)} %my_own.5, ...), custom_call_target="tpu_custom_call" | custom-call | tf_op jit(solution)/shard_map/second/pallas_call | solution.py:494
  61.9 1.9 %collective-permute-start.4 = (f32[4,2,72,512]{3,2,1,0:T(8,128)S(1)}, f32[4,2,72,512]{3,2,1,0:T(8,128)S(1)}, u32[]{:S(2)}, u32[]{:S(2)}) collective-permute-start(f32[4,2,72,512]{3,2,1,0:T(8,128)S(1)} %get-tuple-element.13), channel_id=1, source_target_pairs={{0,1},{1,2},{2,3},{3,4},{4,5},{5,6},{6,7},{7,8},{8,9},{9,10},{10,1... | collective-permute-start | bytes 3538952 | tf_op jit(solution)/shard_map/ppermute | solution.py:427
  63.8 9.9 %third.1 = (f32[4,2,128,512]{3,2,1,0:T(8,128)}, f32[4,2,72,512]{3,2,1,0:T(8,128)S(1)}) custom-call(s32[3]{0:T(128)S(1)} %pad_add_fusion.place, s32[17]{0:T(128)S(1)} %pad_add_fusion.1.mine, s32[17]{0:T(128)S(1)} %collective-permute-done.prev, f32[4,2,128,512]{3,2,1,0:T(8,128)} %my_own.5, f32[4,2,128,512]{3,2,1,0:T(8,128)} %collective-permute-done.1.other_own, ...), custom_call_target="tpu_custom_call" | custom-call | tf_op jit(solution)/shard_map/third/pallas_call | solution.py:508
  73.7 10.8 %collective-permute-done.4 = f32[4,2,72,512]{3,2,1,0:T(8,128)S(1)} collective-permute-done((f32[4,2,72,512]{3,2,1,0:T(8,128)S(1)}, f32[4,2,72,512]{3,2,1,0:T(8,128)S(1)}, u32[]{:S(2)}, u32[]{:S(2)}) %collective-permute-start.4) | collective-permute-done | bytes 1179680 | tf_op jit(solution)/shard_map/ppermute | solution.py:427
  84.5 0.7 add_select_fusion
  85.2 7.2 %collective-permute-start.5 = (f32[4,2,128,512]{3,2,1,0:T(8,128)S(1)}, f32[4,2,128,512]{3,2,1,0:T(8,128)S(1)}, u32[]{:S(2)}, u32[]{:S(2)}) collective-permute-start(f32[4,2,128,512]{3,2,1,0:T(8,128)S(1)} %add_select_fusion), channel_id=1, source_target_pairs={{0,64},{64,0},{1,65},{65,1},{2,66},{66,2},{3,67},{67,3},{4,68},{68... | collective-permute-start | bytes 6291464 | tf_op jit(solution)/shard_map/ppermute | solution.py:431
  92.4 1.3 %collective-permute-start.7 = (f32[4,2,72,512]{3,2,1,0:T(8,128)S(1)}, f32[4,2,72,512]{3,2,1,0:T(8,128)S(1)}, u32[]{:S(2)}, u32[]{:S(2)}) collective-permute-start(f32[4,2,72,512]{3,2,1,0:T(8,128)S(1)} %get-tuple-element.14), channel_id=1, source_target_pairs={{65,0},{66,1},{67,2},{68,3},{69,4},{70,5},{71,6},{72,7},{73,8},{74... | collective-permute-start | bytes 3538952 | tf_op jit(solution)/shard_map/ppermute | solution.py:438
  93.7 1.9 %collective-permute-start.6 = (f32[4,2,72,512]{3,2,1,0:T(8,128)S(1)}, f32[4,2,72,512]{3,2,1,0:T(8,128)S(1)}, u32[]{:S(2)}, u32[]{:S(2)}) collective-permute-start(f32[4,2,72,512]{3,2,1,0:T(8,128)S(1)} %get-tuple-element.14), channel_id=1, source_target_pairs={{0,1},{1,2},{2,3},{3,4},{4,5},{5,6},{6,7},{7,8},{8,9},{9,10},{10,1... | collective-permute-start | bytes 3538952 | tf_op jit(solution)/shard_map/ppermute | solution.py:438
  95.7 14.3 %collective-permute-done.7 = f32[4,2,72,512]{3,2,1,0:T(8,128)S(1)} collective-permute-done((f32[4,2,72,512]{3,2,1,0:T(8,128)S(1)}, f32[4,2,72,512]{3,2,1,0:T(8,128)S(1)}, u32[]{:S(2)}, u32[]{:S(2)}) %collective-permute-start.7) | collective-permute-done | bytes 1179680 | tf_op jit(solution)/shard_map/ppermute | solution.py:438
  109.9 0.1 slice.35
  110.0 0.9 select_add_fusion
  110.9 5.1 %collective-permute-done.6 = f32[4,2,72,512]{3,2,1,0:T(8,128)S(1)} collective-permute-done((f32[4,2,72,512]{3,2,1,0:T(8,128)S(1)}, f32[4,2,72,512]{3,2,1,0:T(8,128)S(1)}, u32[]{:S(2)}, u32[]{:S(2)}) %collective-permute-start.6) | collective-permute-done | bytes 1179680 | tf_op jit(solution)/shard_map/ppermute | solution.py:438
  116.0 1.8 %maximum_add_fusion = f32[4,2,128,512]{3,2,1,0:T(8,128)} fusion(f32[4,2,128,512]{3,2,1,0:T(8,128)S(1)} %select_add_fusion, f32[4,2,56,512]{3,2,1,0:T(8,128)S(1)} %slice.35, f32[4,2,72,512]{3,2,1,0:T(8,128)S(1)} %collective-permute-done.6), kind=kLoop, calls=%fused_computation | loop fusion | flops 1048576 | bytes 6291456 | tf_op jit(solution)/shard_map/add | solution.py:525
  (34 shorter events, 0.1 us)
Async XLA Ops:
  0.0 2.2 %copy-start.3 = (f32[8,128,128]{2,1,0:T(8,128)S(1)}, f32[8,128,128]{2,1,0:T(8,128)}, u32[]{:S(2)}) copy-start(f32[8,128,128]{2,1,0:T(8,128)} %param.11) | copy-start | bytes 1572868
  0.0 4.5 %collective-permute-start.1 = (f32[4,2,128,512]{3,2,1,0:T(8,128)}, f32[4,2,128,512]{3,2,1,0:T(8,128)}, u32[]{:S(2)}, u32[]{:S(2)}) collective-permute-start(f32[4,2,128,512]{3,2,1,0:T(8,128)} %my_own.5), channel_id=1, source_target_pairs={{0,64},{64,0},{1,65},{65,1},{2,66},{66,2},{3,67},{67,3},{4,68},{68... | collective-permute-start | bytes 6291464 | tf_op jit(solution)/shard_map/ppermute | solution.py:431
  2.3 3.5 %copy-start = (f32[4,2,128,512]{3,2,1,0:T(8,128)S(1)}, f32[4,2,128,512]{3,2,1,0:T(8,128)}, u32[]{:S(2)}) copy-start(f32[4,2,128,512]{3,2,1,0:T(8,128)} %my_own.5) | copy-start | bytes 6291460
  5.8 9.8 %copy-start.9 = (f32[4,2,56,512]{3,2,1,0:T(8,128)S(1)}, f32[4,2,56,512]{3,2,1,0:T(8,128)}, u32[]{:S(2)}) copy-start(f32[4,2,56,512]{3,2,1,0:T(8,128)} %slice.29) | copy-start | bytes 2752516
  5.8 9.8 %copy-start.10 = (f32[4,2,16,512]{3,2,1,0:T(8,128)S(1)}, f32[4,2,16,512]{3,2,1,0:T(8,128)}, u32[]{:S(2)}) copy-start(f32[4,2,16,512]{3,2,1,0:T(8,128)} %reshape.18) | copy-start | bytes 786436
  7.0 14.0 %copy-start.12 = (s32[8]{0:T(128)S(1)}, s32[8]{0:T(128)}, u32[]{:S(2)}) copy-start(s32[8]{0:T(128)} %param.13) | copy-start | bytes 100
  7.0 14.0 %copy-start.13 = (s32[8]{0:T(128)S(1)}, s32[8]{0:T(128)}, u32[]{:S(2)}) copy-start(s32[8]{0:T(128)} %param.12) | copy-start | bytes 100
  7.0 14.8 %copy-start.11 = (f32[128,128]{1,0:T(8,128)S(1)}, f32[128,128]{1,0:T(8,128)}, u32[]{:S(2)}) copy-start(f32[128,128]{1,0:T(8,128)} %param.10) | copy-start | bytes 196612
  7.0 22.5 %copy-start.5 = (f32[2,128,128]{2,1,0:T(8,128)S(1)}, f32[2,128,128]{2,1,0:T(8,128)}, u32[]{:S(2)}) copy-start(f32[2,128,128]{2,1,0:T(8,128)} %probe.3) | copy-start | bytes 393220
  7.0 22.5 %collective-permute-start.2 = (f32[4,2,72,512]{3,2,1,0:T(8,128)}, f32[4,2,72,512]{3,2,1,0:T(8,128)S(1)}, u32[]{:S(2)}, u32[]{:S(2)}) collective-permute-start(f32[4,2,72,512]{3,2,1,0:T(8,128)} %maximum_select_fusion), channel_id=1, source_target_pairs={{1,0},{2,1},{3,2},{4,3},{5,4},{6,5},{7,6},{8,7},{9,8},{10,9},{11,1... | collective-permute-start | bytes 3538952 | tf_op jit(solution)/shard_map/ppermute | solution.py:427
  18.1 24.1 %collective-permute-start.3 = (f32[4,2,72,512]{3,2,1,0:T(8,128)}, f32[4,2,72,512]{3,2,1,0:T(8,128)}, u32[]{:S(2)}, u32[]{:S(2)}) collective-permute-start(f32[4,2,72,512]{3,2,1,0:T(8,128)} %slice_select_fusion), channel_id=1, source_target_pairs={{1,0},{2,1},{3,2},{4,3},{5,4},{6,5},{7,6},{8,7},{9,8},{10,9},{11,1... | collective-permute-start | bytes 3538952 | tf_op jit(solution)/shard_map/ppermute | solution.py:427
  21.1 1.0 collective-permute-start
  29.6 1.0 copy-start.1
  30.6 11.6 %copy-start.2 = (bf16[2,2,256,256]{3,2,1,0:T(8,128)(2,1)S(1)}, bf16[2,2,256,256]{3,2,1,0:T(8,128)(2,1)}, u32[]{:S(2)}) copy-start(bf16[2,2,256,256]{3,2,1,0:T(8,128)(2,1)} %constant.18.clone.tab) | copy-start | bytes 1572868
  30.6 11.6 %copy-start.4 = (f32[8,128,128]{2,1,0:T(8,128)S(1)}, f32[8,128,128]{2,1,0:T(8,128)}, u32[]{:S(2)}) copy-start(f32[8,128,128]{2,1,0:T(8,128)} %param.11) | copy-start | bytes 1572868
  61.9 22.7 %collective-permute-start.4 = (f32[4,2,72,512]{3,2,1,0:T(8,128)S(1)}, f32[4,2,72,512]{3,2,1,0:T(8,128)S(1)}, u32[]{:S(2)}, u32[]{:S(2)}) collective-permute-start(f32[4,2,72,512]{3,2,1,0:T(8,128)S(1)} %get-tuple-element.13), channel_id=1, source_target_pairs={{0,1},{1,2},{2,3},{3,4},{4,5},{5,6},{6,7},{7,8},{8,9},{9,10},{10,1... | collective-permute-start | bytes 3538952 | tf_op jit(solution)/shard_map/ppermute | solution.py:427
  63.8 20.7 %copy-start.6 = (f32[4,2,128,512]{3,2,1,0:T(8,128)S(1)}, f32[4,2,128,512]{3,2,1,0:T(8,128)}, u32[]{:S(2)}) copy-start(f32[4,2,128,512]{3,2,1,0:T(8,128)} %get-tuple-element.12) | copy-start | bytes 6291460
  84.5 11.1 %copy-start.8 = (f32[4,2,72,512]{3,2,1,0:T(8,128)}, f32[4,2,72,512]{3,2,1,0:T(8,128)S(1)}, u32[]{:S(2)}) copy-start(f32[4,2,72,512]{3,2,1,0:T(8,128)S(1)} %collective-permute-done.4) | copy-start | bytes 3538948
  85.2 24.8 %copy-start.7 = (f32[4,2,128,512]{3,2,1,0:T(8,128)S(1)}, f32[4,2,128,512]{3,2,1,0:T(8,128)}, u32[]{:S(2)}) copy-start(f32[4,2,128,512]{3,2,1,0:T(8,128)} %get-tuple-element.11) | copy-start | bytes 6291460
  85.2 24.8 %collective-permute-start.5 = (f32[4,2,128,512]{3,2,1,0:T(8,128)S(1)}, f32[4,2,128,512]{3,2,1,0:T(8,128)S(1)}, u32[]{:S(2)}, u32[]{:S(2)}) collective-permute-start(f32[4,2,128,512]{3,2,1,0:T(8,128)S(1)} %add_select_fusion), channel_id=1, source_target_pairs={{0,64},{64,0},{1,65},{65,1},{2,66},{66,2},{3,67},{67,3},{4,68},{68... | collective-permute-start | bytes 6291464 | tf_op jit(solution)/shard_map/ppermute | solution.py:431
  92.4 17.5 %collective-permute-start.7 = (f32[4,2,72,512]{3,2,1,0:T(8,128)S(1)}, f32[4,2,72,512]{3,2,1,0:T(8,128)S(1)}, u32[]{:S(2)}, u32[]{:S(2)}) collective-permute-start(f32[4,2,72,512]{3,2,1,0:T(8,128)S(1)} %get-tuple-element.14), channel_id=1, source_target_pairs={{65,0},{66,1},{67,2},{68,3},{69,4},{70,5},{71,6},{72,7},{73,8},{74... | collective-permute-start | bytes 3538952 | tf_op jit(solution)/shard_map/ppermute | solution.py:438
  93.7 22.3 %collective-permute-start.6 = (f32[4,2,72,512]{3,2,1,0:T(8,128)S(1)}, f32[4,2,72,512]{3,2,1,0:T(8,128)S(1)}, u32[]{:S(2)}, u32[]{:S(2)}) collective-permute-start(f32[4,2,72,512]{3,2,1,0:T(8,128)S(1)} %get-tuple-element.14), channel_id=1, source_target_pairs={{0,1},{1,2},{2,3},{3,4},{4,5},{5,6},{6,7},{7,8},{8,9},{9,10},{10,1... | collective-permute-start | bytes 3538952 | tf_op jit(solution)/shard_map/ppermute | solution.py:438
  95.7 14.4 %slice-start = ((f32[4,2,72,512]{3,2,1,0:T(8,128)}), f32[4,2,56,512]{3,2,1,0:T(8,128)S(1)}, s32[]{:S(2)}) async-start(f32[4,2,72,512]{3,2,1,0:T(8,128)} %copy-done.8), calls=%async_computation | async-start | bytes 1835008 | tf_op jit(solution)/shard_map/slice | solution.py:522

commit v3 on v2

--- a/solution.py
+++ b/solution.py
@@ -463,7 +463,10 @@
     other = partner(specimen_layers)
     prev = strips(mine, 1, 1, 1)
     low = packed(depth, specimen_layers, other, recorded_intensities[:4])
-    high = packed(depth, other, specimen_layers, recorded_intensities[4:])
+    late_own, late_other, late_ints, low = lax.optimization_barrier(
+        (specimen_layers, other, recorded_intensities[4:], low)
+    )
+    high = packed(depth, late_other, late_own, late_ints)
     low_rim = both_ways(low, False)
     high_rim = both_ways(high, False)
     H = jnp.stack([jnp.cos(propagator_spectral_angle), jnp.sin(propagator_spectral_angle)])

time: 119 us -> 120 us (level)
  waiting for transfers between devices: 40.2 us -> 42.2 us
    slice x2, local copies, waits for them, and re-layouts: 3.48 us -> 1.3 us  [packed(): below[:, :, RIM:]]
    ppermute x2, waiting for transfers between devices: 0.91 us -> 2.99 us  [partner(): return lax.ppermute(value, 'depth', [(0, 1), (1, 0)])]
  transfers between devices with their start and end apart: 8 -> 8, of which waited for: 6 -> 6; matrix products, arithmetic and copies ran while one was open for 6% -> 5% of each run, Pallas kernels for 17% -> 17%
where the time goes in v3:
time: 120 us; the launch traced here: 119 us
  waiting for transfers between devices  42.2 us (35%)
  Pallas kernels  39.4 us (33%)
  starting transfers between devices  23.8 us (20%)
  other arithmetic  7.37 us (6%)
  local copies, waits for them, and re-layouts  5.18 us (4%)
    ppermute x3, waiting for transfers between devices, both_ways(): return lax.ppermute(value, ('depth', 'tile'), pairs)  19.8 us
    pallas_call x1, Pallas kernels, local(): pl.pallas_call(second_kernel, out_shape=[own, rim, errors], in_specs=[sm]...  19.7 us
    ppermute x3, waiting for transfers between devices, strips(): return lax.ppermute(value, ('depth', 'tile'), pairs)  19.4 us
    ppermute x3, starting transfers between devices, both_ways(): return lax.ppermute(value, ('depth', 'tile'), pairs)  12.7 us
    pallas_call x1, Pallas kernels, local(): pl.pallas_call(third_kernel, out_shape=[own, rim], in_specs=[sm] * 3 + [h...  9.93 us
    pallas_call x1, Pallas kernels, local(): pl.pallas_call(first_kernel, out_shape=jax.ShapeDtypeStruct((GROUP, SLOTS...  9.85 us
    ppermute x2, starting transfers between devices, partner(): return lax.ppermute(value, 'depth', [(0, 1), (1, 0)])  7.24 us
    select_n x2, other arithmetic, packed(): jnp.where(depth == 0, above[:, :, :RIM], jnp.concatenate([side, below[:,...  3.87 us
  transfers between devices with their start and end apart: 8, of which 6 were waited for; matrix products, arithmetic and copies ran while one was open for 5% of the time, Pallas kernels for 17%

profile of v3, /device:TPU:2, one launch (start us, length us, event | category | flops | bytes accessed | tf_op | source)
XLA Modules:
  0.0 118.9 jit_solution(10442748012839476930)
XLA Ops:
  0.0 1.2 %fusion = (f32[4,128,128]{2,1,0:T(8,128)S(1)}, f32[4,128,128]{2,1,0:T(8,128)S(1)}) fusion(f32[8,128,128]{2,1,0:T(8,128)} %param.11), kind=kLoop, calls=%fused_computation.12 | loop fusion | bytes 1048576 | tf_op jit(solution)/shard_map/slice | solution.py:465
  1.2 0.2 copy.14
  1.4 0.1 reshape.16
  1.5 3.0 %collective-permute-done.1.other_own = f32[4,2,128,512]{3,2,1,0:T(8,128)} collective-permute-done((f32[4,2,128,512]{3,2,1,0:T(8,128)}, f32[4,2,128,512]{3,2,1,0:T(8,128)}, u32[]{:S(2)}, u32[]{:S(2)}) %collective-permute-start.1) | collective-permute-done | bytes 2097184 | tf_op jit(solution)/shard_map/ppermute | solution.py:431
  4.5 1.2 %slice.32 = f32[4,2,56,512]{3,2,1,0:T(8,128)S(1)} slice(f32[4,2,128,512]{3,2,1,0:T(8,128)} %collective-permute-done.1.other_own), slice={[0:4], [0:2], [72:128], [0:512]} | slice | bytes 1835008 | tf_op jit(solution)/shard_map/slice | solution.py:444
  5.8 1.3 %maximum_select_fusion = f32[4,2,72,512]{3,2,1,0:T(8,128)} fusion(f32[4,2,56,512]{3,2,1,0:T(8,128)S(1)} %slice.32, f32[4,2,16,512]{3,2,1,0:T(8,128)S(1)} %reshape.16, f32[4,2,128,512]{3,2,1,0:T(8,128)S(1)} %copy-done, pred[]{:T(512)S(6)} %eq.2), kind=kLoop, calls=%fused_computation.3 | loop fusion | flops 589824 | bytes 3538945 | tf_op jit(solution)/shard_map/jit(_where)/select_n | solution.py:443
  7.0 0.2 copy.13
  7.2 0.8 reshape.18
  8.0 0.1 slice.29
  8.1 8.5 %collective-permute-start.2 = (f32[4,2,72,512]{3,2,1,0:T(8,128)}, f32[4,2,72,512]{3,2,1,0:T(8,128)S(1)}, u32[]{:S(2)}, u32[]{:S(2)}) collective-permute-start(f32[4,2,72,512]{3,2,1,0:T(8,128)} %maximum_select_fusion), channel_id=1, source_target_pairs={{1,0},{2,1},{3,2},{4,3},{5,4},{6,5},{7,6},{8,7},{9,8},{10,9},{11,1... | collective-permute-start | bytes 3538952 | tf_op jit(solution)/shard_map/ppermute | solution.py:427
  16.6 2.6 %maximum_select_fusion.1 = f32[4,2,72,512]{3,2,1,0:T(8,128)} fusion(f32[4,2,56,512]{3,2,1,0:T(8,128)S(1)} %slice.29, f32[4,2,16,512]{3,2,1,0:T(8,128)} %reshape.18, f32[4,2,128,512]{3,2,1,0:T(8,128)} %collective-permute-done.1.other_own, pred[]{:T(512)S(6)} %eq.2), kind=kLoop, calls=%fused_computation.4 | loop fusion | flops 589824 | bytes 3538945 | tf_op jit(solution)/shard_map/jit(_where)/select_n | solution.py:443
  19.2 2.3 %collective-permute-start.3 = (f32[4,2,72,512]{3,2,1,0:T(8,128)}, f32[4,2,72,512]{3,2,1,0:T(8,128)}, u32[]{:S(2)}, u32[]{:S(2)}) collective-permute-start(f32[4,2,72,512]{3,2,1,0:T(8,128)} %maximum_select_fusion.1), channel_id=1, source_target_pairs={{1,0},{2,1},{3,2},{4,3},{5,4},{6,5},{7,6},{8,7},{9,8},{10,9},{11,1... | collective-permute-start | bytes 3538952 | tf_op jit(solution)/shard_map/ppermute | solution.py:427
  22.2 0.1 pad_add_fusion.1.mine
  22.3 0.7 collective-permute-start
  23.0 0.2 cosine_bitcast_fusion
  23.2 0.1 pad_add_fusion.place
  23.3 7.3 %collective-permute-done.2.rim.low_rim = f32[4,2,72,512]{3,2,1,0:T(8,128)S(1)} collective-permute-done((f32[4,2,72,512]{3,2,1,0:T(8,128)}, f32[4,2,72,512]{3,2,1,0:T(8,128)S(1)}, u32[]{:S(2)}, u32[]{:S(2)}) %collective-permute-start.2) | collective-permute-done | bytes 1179680 | tf_op jit(solution)/shard_map/ppermute | solution.py:427
  30.6 1.0 copy-done.1
  31.7 9.8 %first.1.psi = f32[4,1024,256]{2,1,0:T(8,128)} custom-call(s32[3]{0:T(128)S(1)} %pad_add_fusion.place, s32[17]{0:T(128)S(1)} %pad_add_fusion.1.mine, s32[17]{0:T(128)S(1)} %collective-permute-done.prev, f32[4,2,128,512]{3,2,1,0:T(8,128)S(1)} %copy-done, f32[4,2,128,512]{3,2,1,0:T(8,128)} %collective-permute-done.1.other_own, ...), custom_call_target="tpu_custom_call" | custom-call | tf_op jit(solution)/shard_map/first/pallas_call | solution.py:488
  41.6 1.7 %collective-permute-done.3.rim = f32[4,2,72,512]{3,2,1,0:T(8,128)} collective-permute-done((f32[4,2,72,512]{3,2,1,0:T(8,128)}, f32[4,2,72,512]{3,2,1,0:T(8,128)}, u32[]{:S(2)}, u32[]{:S(2)}) %collective-permute-start.3) | collective-permute-done | bytes 1179680 | tf_op jit(solution)/shard_map/ppermute | solution.py:427
  43.3 19.7 %second.1 = (f32[4,2,128,512]{3,2,1,0:T(8,128)}, f32[4,2,72,512]{3,2,1,0:T(8,128)S(1)}, f32[1024,256]{1,0:T(8,128)S(1)}) custom-call(s32[3]{0:T(128)S(1)} %pad_add_fusion.place, s32[17]{0:T(128)S(1)} %pad_add_fusion.1.mine, s32[17]{0:T(128)S(1)} %collective-permute-done.prev, f32[4,2,128,512]{3,2,1,0:T(8,128)} %my_own.5, ...), custom_call_target="tpu_custom_call" | custom-call | tf_op jit(solution)/shard_map/second/pallas_call | solution.py:497
  63.0 1.9 %collective-permute-start.4 = (f32[4,2,72,512]{3,2,1,0:T(8,128)S(1)}, f32[4,2,72,512]{3,2,1,0:T(8,128)S(1)}, u32[]{:S(2)}, u32[]{:S(2)}) collective-permute-start(f32[4,2,72,512]{3,2,1,0:T(8,128)S(1)} %get-tuple-element.21), channel_id=1, source_target_pairs={{0,1},{1,2},{2,3},{3,4},{4,5},{5,6},{6,7},{7,8},{8,9},{9,10},{10,1... | collective-permute-start | bytes 3538952 | tf_op jit(solution)/shard_map/ppermute | solution.py:427
  64.9 9.9 %third.1 = (f32[4,2,128,512]{3,2,1,0:T(8,128)}, f32[4,2,72,512]{3,2,1,0:T(8,128)S(1)}) custom-call(s32[3]{0:T(128)S(1)} %pad_add_fusion.place, s32[17]{0:T(128)S(1)} %pad_add_fusion.1.mine, s32[17]{0:T(128)S(1)} %collective-permute-done.prev, f32[4,2,128,512]{3,2,1,0:T(8,128)} %my_own.5, f32[4,2,128,512]{3,2,1,0:T(8,128)} %collective-permute-done.1.other_own, ...), custom_call_target="tpu_custom_call" | custom-call | tf_op jit(solution)/shard_map/third/pallas_call | solution.py:511
  74.8 10.8 %collective-permute-done.4 = f32[4,2,72,512]{3,2,1,0:T(8,128)S(1)} collective-permute-done((f32[4,2,72,512]{3,2,1,0:T(8,128)S(1)}, f32[4,2,72,512]{3,2,1,0:T(8,128)S(1)}, u32[]{:S(2)}, u32[]{:S(2)}) %collective-permute-start.4) | collective-permute-done | bytes 1179680 | tf_op jit(solution)/shard_map/ppermute | solution.py:427
  85.6 0.7 add_select_fusion
  86.3 7.2 %collective-permute-start.5 = (f32[4,2,128,512]{3,2,1,0:T(8,128)S(1)}, f32[4,2,128,512]{3,2,1,0:T(8,128)S(1)}, u32[]{:S(2)}, u32[]{:S(2)}) collective-permute-start(f32[4,2,128,512]{3,2,1,0:T(8,128)S(1)} %add_select_fusion), channel_id=1, source_target_pairs={{0,64},{64,0},{1,65},{65,1},{2,66},{66,2},{3,67},{67,3},{4,68},{68... | collective-permute-start | bytes 6291464 | tf_op jit(solution)/shard_map/ppermute | solution.py:431
  93.5 1.3 %collective-permute-start.7 = (f32[4,2,72,512]{3,2,1,0:T(8,128)S(1)}, f32[4,2,72,512]{3,2,1,0:T(8,128)S(1)}, u32[]{:S(2)}, u32[]{:S(2)}) collective-permute-start(f32[4,2,72,512]{3,2,1,0:T(8,128)S(1)} %get-tuple-element.22), channel_id=1, source_target_pairs={{65,0},{66,1},{67,2},{68,3},{69,4},{70,5},{71,6},{72,7},{73,8},{74... | collective-permute-start | bytes 3538952 | tf_op jit(solution)/shard_map/ppermute | solution.py:438
  94.8 1.9 %collective-permute-start.6 = (f32[4,2,72,512]{3,2,1,0:T(8,128)S(1)}, f32[4,2,72,512]{3,2,1,0:T(8,128)S(1)}, u32[]{:S(2)}, u32[]{:S(2)}) collective-permute-start(f32[4,2,72,512]{3,2,1,0:T(8,128)S(1)} %get-tuple-element.22), channel_id=1, source_target_pairs={{0,1},{1,2},{2,3},{3,4},{4,5},{5,6},{6,7},{7,8},{8,9},{9,10},{10,1... | collective-permute-start | bytes 3538952 | tf_op jit(solution)/shard_map/ppermute | solution.py:438
  96.8 14.3 %collective-permute-done.7 = f32[4,2,72,512]{3,2,1,0:T(8,128)S(1)} collective-permute-done((f32[4,2,72,512]{3,2,1,0:T(8,128)S(1)}, f32[4,2,72,512]{3,2,1,0:T(8,128)S(1)}, u32[]{:S(2)}, u32[]{:S(2)}) %collective-permute-start.7) | collective-permute-done | bytes 1179680 | tf_op jit(solution)/shard_map/ppermute | solution.py:438
  111.1 0.9 select_add_fusion
  112.0 5.1 %collective-permute-done.6 = f32[4,2,72,512]{3,2,1,0:T(8,128)S(1)} collective-permute-done((f32[4,2,72,512]{3,2,1,0:T(8,128)S(1)}, f32[4,2,72,512]{3,2,1,0:T(8,128)S(1)}, u32[]{:S(2)}, u32[]{:S(2)}) %collective-permute-start.6) | collective-permute-done | bytes 1179680 | tf_op jit(solution)/shard_map/ppermute | solution.py:438
  117.1 1.8 %maximum_add_fusion = f32[4,2,128,512]{3,2,1,0:T(8,128)} fusion(f32[4,2,128,512]{3,2,1,0:T(8,128)S(1)} %select_add_fusion, f32[4,2,56,512]{3,2,1,0:T(8,128)S(1)} %slice.34, f32[4,2,72,512]{3,2,1,0:T(8,128)S(1)} %collective-permute-done.6), kind=kLoop, calls=%fused_computation | loop fusion | flops 1048576 | bytes 6291456 | tf_op jit(solution)/shard_map/add | solution.py:528
  (28 shorter events, 0.1 us)
Async XLA Ops:
  0.0 5.7 %copy-start = (f32[4,2,128,512]{3,2,1,0:T(8,128)S(1)}, f32[4,2,128,512]{3,2,1,0:T(8,128)}, u32[]{:S(2)}) copy-start(f32[4,2,128,512]{3,2,1,0:T(8,128)} %my_own.5) | copy-start | bytes 6291460
  0.0 4.5 %collective-permute-start.1 = (f32[4,2,128,512]{3,2,1,0:T(8,128)}, f32[4,2,128,512]{3,2,1,0:T(8,128)}, u32[]{:S(2)}, u32[]{:S(2)}) collective-permute-start(f32[4,2,128,512]{3,2,1,0:T(8,128)} %my_own.5), channel_id=1, source_target_pairs={{0,64},{64,0},{1,65},{65,1},{2,66},{66,2},{3,67},{67,3},{4,68},{68... | collective-permute-start | bytes 6291464 | tf_op jit(solution)/shard_map/ppermute | solution.py:431
  8.1 14.1 %copy-start.9 = (s32[8]{0:T(128)S(1)}, s32[8]{0:T(128)}, u32[]{:S(2)}) copy-start(s32[8]{0:T(128)} %param.13) | copy-start | bytes 100
  8.1 14.1 %copy-start.10 = (s32[8]{0:T(128)S(1)}, s32[8]{0:T(128)}, u32[]{:S(2)}) copy-start(s32[8]{0:T(128)} %param.12) | copy-start | bytes 100
  8.1 14.9 %copy-start.8 = (f32[128,128]{1,0:T(8,128)S(1)}, f32[128,128]{1,0:T(8,128)}, u32[]{:S(2)}) copy-start(f32[128,128]{1,0:T(8,128)} %param.10) | copy-start | bytes 196612
  8.1 22.5 %copy-start.4 = (f32[2,128,128]{2,1,0:T(8,128)S(1)}, f32[2,128,128]{2,1,0:T(8,128)}, u32[]{:S(2)}) copy-start(f32[2,128,128]{2,1,0:T(8,128)} %probe.3) | copy-start | bytes 393220
  8.1 22.5 %collective-permute-start.2 = (f32[4,2,72,512]{3,2,1,0:T(8,128)}, f32[4,2,72,512]{3,2,1,0:T(8,128)S(1)}, u32[]{:S(2)}, u32[]{:S(2)}) collective-permute-start(f32[4,2,72,512]{3,2,1,0:T(8,128)} %maximum_select_fusion), channel_id=1, source_target_pairs={{1,0},{2,1},{3,2},{4,3},{5,4},{6,5},{7,6},{8,7},{9,8},{10,9},{11,1... | collective-permute-start | bytes 3538952 | tf_op jit(solution)/shard_map/ppermute | solution.py:427
  19.2 24.0 %collective-permute-start.3 = (f32[4,2,72,512]{3,2,1,0:T(8,128)}, f32[4,2,72,512]{3,2,1,0:T(8,128)}, u32[]{:S(2)}, u32[]{:S(2)}) collective-permute-start(f32[4,2,72,512]{3,2,1,0:T(8,128)} %maximum_select_fusion.1), channel_id=1, source_target_pairs={{1,0},{2,1},{3,2},{4,3},{5,4},{6,5},{7,6},{8,7},{9,8},{10,9},{11,1... | collective-permute-start | bytes 3538952 | tf_op jit(solution)/shard_map/ppermute | solution.py:427
  22.3 1.0 collective-permute-start
  30.6 1.0 copy-start.1
  31.7 11.6 %copy-start.2 = (bf16[2,2,256,256]{3,2,1,0:T(8,128)(2,1)S(1)}, bf16[2,2,256,256]{3,2,1,0:T(8,128)(2,1)}, u32[]{:S(2)}) copy-start(bf16[2,2,256,256]{3,2,1,0:T(8,128)(2,1)} %constant.18.clone.tab) | copy-start | bytes 1572868
  31.7 11.6 %copy-start.3 = (f32[8,128,128]{2,1,0:T(8,128)S(1)}, f32[8,128,128]{2,1,0:T(8,128)}, u32[]{:S(2)}) copy-start(f32[8,128,128]{2,1,0:T(8,128)} %param.11) | copy-start | bytes 1572868
  63.0 22.6 %collective-permute-start.4 = (f32[4,2,72,512]{3,2,1,0:T(8,128)S(1)}, f32[4,2,72,512]{3,2,1,0:T(8,128)S(1)}, u32[]{:S(2)}, u32[]{:S(2)}) collective-permute-start(f32[4,2,72,512]{3,2,1,0:T(8,128)S(1)} %get-tuple-element.21), channel_id=1, source_target_pairs={{0,1},{1,2},{2,3},{3,4},{4,5},{5,6},{6,7},{7,8},{8,9},{9,10},{10,1... | collective-permute-start | bytes 3538952 | tf_op jit(solution)/shard_map/ppermute | solution.py:427
  64.9 20.7 %copy-start.5 = (f32[4,2,128,512]{3,2,1,0:T(8,128)S(1)}, f32[4,2,128,512]{3,2,1,0:T(8,128)}, u32[]{:S(2)}) copy-start(f32[4,2,128,512]{3,2,1,0:T(8,128)} %get-tuple-element.20) | copy-start | bytes 6291460
  85.6 11.1 %copy-start.7 = (f32[4,2,72,512]{3,2,1,0:T(8,128)}, f32[4,2,72,512]{3,2,1,0:T(8,128)S(1)}, u32[]{:S(2)}) copy-start(f32[4,2,72,512]{3,2,1,0:T(8,128)S(1)} %collective-permute-done.4) | copy-start | bytes 3538948
  86.3 24.8 %copy-start.6 = (f32[4,2,128,512]{3,2,1,0:T(8,128)S(1)}, f32[4,2,128,512]{3,2,1,0:T(8,128)}, u32[]{:S(2)}) copy-start(f32[4,2,128,512]{3,2,1,0:T(8,128)} %get-tuple-element.19) | copy-start | bytes 6291460
  86.3 24.8 %collective-permute-start.5 = (f32[4,2,128,512]{3,2,1,0:T(8,128)S(1)}, f32[4,2,128,512]{3,2,1,0:T(8,128)S(1)}, u32[]{:S(2)}, u32[]{:S(2)}) collective-permute-start(f32[4,2,128,512]{3,2,1,0:T(8,128)S(1)} %add_select_fusion), channel_id=1, source_target_pairs={{0,64},{64,0},{1,65},{65,1},{2,66},{66,2},{3,67},{67,3},{4,68},{68... | collective-permute-start | bytes 6291464 | tf_op jit(solution)/shard_map/ppermute | solution.py:431
  93.5 17.5 %collective-permute-start.7 = (f32[4,2,72,512]{3,2,1,0:T(8,128)S(1)}, f32[4,2,72,512]{3,2,1,0:T(8,128)S(1)}, u32[]{:S(2)}, u32[]{:S(2)}) collective-permute-start(f32[4,2,72,512]{3,2,1,0:T(8,128)S(1)} %get-tuple-element.22), channel_id=1, source_target_pairs={{65,0},{66,1},{67,2},{68,3},{69,4},{70,5},{71,6},{72,7},{73,8},{74... | collective-permute-start | bytes 3538952 | tf_op jit(solution)/shard_map/ppermute | solution.py:438
  94.8 22.3 %collective-permute-start.6 = (f32[4,2,72,512]{3,2,1,0:T(8,128)S(1)}, f32[4,2,72,512]{3,2,1,0:T(8,128)S(1)}, u32[]{:S(2)}, u32[]{:S(2)}) collective-permute-start(f32[4,2,72,512]{3,2,1,0:T(8,128)S(1)} %get-tuple-element.22), channel_id=1, source_target_pairs={{0,1},{1,2},{2,3},{3,4},{4,5},{5,6},{6,7},{7,8},{8,9},{9,10},{10,1... | collective-permute-start | bytes 3538952 | tf_op jit(solution)/shard_map/ppermute | solution.py:438
  96.7 14.4 %slice-start = ((f32[4,2,72,512]{3,2,1,0:T(8,128)}), f32[4,2,56,512]{3,2,1,0:T(8,128)S(1)}, s32[]{:S(2)}) async-start(f32[4,2,72,512]{3,2,1,0:T(8,128)} %copy-done.7), calls=%async_computation | async-start | bytes 1835008 | tf_op jit(solution)/shard_map/slice | solution.py:525
